TPU v7x, 32 devices: a whole 2x2x4 slice. The times are simulated.
32 devices in a mesh: row: 16 (over z, y, x), col: 2 (over core).
Axes of the slice: x: 2, y: 2, z: 4, core: 2. Of those that a mesh axis runs over, the one named last changes fastest.
Arguments:
- blocks: float32 [16, 2, 40, 128, 128], P('row', 'col'), may hold values from -0.078125 to 0.078125
- block_rows: int32 [16, 2, 40], P('row', 'col'), may hold values from 0 to 15
- block_cols: int32 [16, 2, 40], P(None, 'col'), may hold values from 0 to 127, as said below
- start_basis: float32 [32, 32768], P(None, ('row', 'col')), may hold values from -6 to 6
- targets: int32 [16], replicated, may hold values from 0 to 31, as said below
Outputs:
- right_basis: float32 [32, 32768], P(None, ('row', 'col'))
- left_basis: float32 [32, 32768], P(None, ('row', 'col'))
- triangle: float32 [32, 32], replicated
Inputs may be any that keep to these rules, and one draw needn't show every extreme that they name: For every r, c and o < 16, all entries block_cols[r, c, n] with block_cols[r, c, n] // 8 = o are equal. `targets`: 16 distinct indices.
All inputs are finite; a program needn't handle non-finite values.
Results may differ from a plain program's by a relative error of at most 0.0001.
Values sent between devices are 32-bit elements; how exact they have to be, the bound alone decides.
No kernel may reach another device: no remote copies, remote signals or barrier semaphores. Data moves between devices by JAX's collectives and lax.ppermute only.
A program may use at most 64 MiB of HBM per device.

v0:
```python
import jax
import jax.numpy as jnp
from jax import lax
from jax.sharding import PartitionSpec as P

OUTER = 2
INNER = 4


highest = lax.Precision.HIGHEST


def lower_solve(lower, vectors):
    return lax.linalg.triangular_solve(lower, vectors, left_side=True, lower=True)


def gram_local(vectors):
    return jnp.dot(vectors, vectors.T, precision=highest)


def basis_factor(trial_basis, total_rows):
    gram_sum = lax.psum(gram_local(trial_basis), ("row", "col"))
    return jnp.linalg.cholesky(gram_sum / total_rows)


def multiply(vectors, block_tiles, tables):
    pick_hot, owners_mine, owner_hot, row_hot, rows_local = tables
    count_vectors = vectors.shape[0]
    block_size = block_tiles.shape[-1]
    segments = vectors.reshape(count_vectors, -1, block_size)
    outgoing = jnp.einsum("rt,ktb->rkb", pick_hot, segments, precision=highest)
    incoming = lax.all_to_all(outgoing, "row", split_axis=0, concat_axis=0, tiled=True)
    picked = incoming[owners_mine]
    products = jnp.einsum("nij,nkj->kni", block_tiles, picked, precision=highest)
    partial_value = jnp.einsum("nr,kni->kri", row_hot, products, precision=highest).reshape(
        count_vectors, -1
    )
    own_rows = lax.psum_scatter(partial_value, "col", scatter_dimension=1, tiled=True)
    result = (own_rows, own_rows)
    return result


def multiply_back(left_rows, block_tiles, tables):
    pick_hot, owners_mine, owner_hot, row_hot, rows_local = tables
    count_vectors = left_rows.shape[0]
    block_size = block_tiles.shape[-1]
    segments = left_rows.reshape(count_vectors, -1, block_size)
    picked = segments[:, rows_local]
    products = jnp.einsum("nij,kni->knj", block_tiles, picked, precision=highest)
    outgoing = jnp.einsum("no,knj->okj", owner_hot, products, precision=highest)
    incoming = lax.all_to_all(outgoing, "row", split_axis=0, concat_axis=0, tiled=True)
    returned = jnp.einsum("rt,rkb->ktb", pick_hot, incoming, precision=highest)
    return returned.reshape(count_vectors, -1)


def shards(blocks, block_rows, block_cols, start_basis, targets):
    block_size = blocks.shape[-1]
    block_tiles = blocks.reshape(-1, block_size, block_size)
    rows_local = block_rows.reshape(-1)
    row_count = lax.axis_size("row")
    col_count = lax.axis_size("col")
    own_width = start_basis.shape[1]
    seg_count = own_width // block_size
    total_rows = float(own_width * row_count * col_count)
    count_vectors = start_basis.shape[0]
    pattern = block_cols[:, 0, :]
    me_row = lax.axis_index("row")
    cols_local = lax.dynamic_index_in_dim(pattern, me_row, 0, keepdims=False)
    owners_mine = cols_local // seg_count
    seg_ids = jnp.arange(seg_count, dtype=jnp.int32)
    matched = pattern // seg_count == me_row
    within = pattern % seg_count
    pick_hot = jnp.any(
        matched[:, :, None] & (within[:, :, None] == seg_ids[None, None, :]), axis=1
    ).astype(jnp.float32)
    owner_hot = (owners_mine[:, None] == jnp.arange(row_count, dtype=jnp.int32)[None, :]).astype(
        jnp.float32
    )
    row_hot = (
        rows_local[:, None] == jnp.arange(col_count * seg_count, dtype=jnp.int32)[None, :]
    ).astype(jnp.float32)
    col_hot = (
        cols_local[:, None] == jnp.arange(row_count * seg_count, dtype=jnp.int32)[None, :]
    ).astype(jnp.float32)
    tables = (pick_hot, owners_mine, owner_hot, row_hot, rows_local)
    squared = jnp.sum(block_tiles * block_tiles, axis=1)
    column_terms = jnp.dot(col_hot.T, squared, precision=highest).reshape(-1)
    squares = lax.psum_scatter(column_terms, "row", scatter_dimension=0, tiled=True)
    largest = lax.pmax(jnp.max(squares), ("row", "col"))
    chosen = jnp.sum(
        (targets[None, :] == jnp.arange(count_vectors, dtype=jnp.int32)[:, None]).astype(
            jnp.float32
        ),
        axis=1,
    )
    trial_basis = start_basis
    left_own = start_basis
    lower_image = jnp.zeros((count_vectors, count_vectors), jnp.float32)
    for outer_step in range(OUTER):
        lower_basis = basis_factor(trial_basis, total_rows)
        right_now = lower_solve(lower_basis, trial_basis)
        image_own, image_rows = multiply(right_now, block_tiles, tables)
        gram_image = lax.psum(gram_local(image_own), ("row", "col"))
        lower_image = jnp.linalg.cholesky(gram_image / total_rows)
        left_own = lower_solve(lower_image, image_own)
        left_rows = lax.all_gather(left_own, "col", axis=1, tiled=True)
        back_own = multiply_back(left_rows, block_tiles, tables)
        residual = back_own - jnp.dot(lower_image.T, right_now, precision=highest)
        shifts = jnp.sum(lower_image * lower_image, axis=1) + largest
        correction = residual / shifts[:, None]
        for inner_step in range(1, INNER):
            coupling = (
                lax.psum(
                    jnp.dot(right_now, (squares[None, :] * correction).T, precision=highest),
                    ("row", "col"),
                )
                / total_rows
            )
            correction = (
                residual
                + squares[None, :] * correction
                - jnp.dot(coupling.T, right_now, precision=highest)
            ) / shifts[:, None]
        trial_basis = right_now + chosen[:, None] * correction
    lower_basis = basis_factor(trial_basis, total_rows)
    return (lower_solve(lower_basis, trial_basis), left_own, lower_image.T)


def solution(mesh):
    in_specs = (
        P("row", "col", None, None, None),
        P("row", "col", None),
        P(None, "col", None),
        P(None, ("row", "col")),
        P(),
    )
    out_specs = (P(None, ("row", "col")), P(None, ("row", "col")), P())
    return jax.shard_map(shards, mesh=mesh, in_specs=in_specs, out_specs=out_specs, check_vma=False)
```

profile of v0, /device:TPU:0, one launch (start us, length us, event | category | flops | bytes accessed | tf_op | source)
XLA Modules:
  0.0 756.0 jit_solution(7076702651899851333)
XLA Ops:
  8.0 0.9 add_select_fusion
  8.9 0.7 fusion.97
  9.9 42.1 %psum.77 = f32[32,32]{0,1:T(8,128)S(1)} all-reduce(f32[32,32]{0,1:T(8,128)S(1)} %fusion.142), channel_id=1, replica_groups=mesh['row'=16,'col'=2] {'row','col'}, use_global_device_ids=true, to_apply=%region_0.1 | all-reduce | flops 1024 | bytes 8192 | tf_op jit(solution)/shard_map/psum | solution.py:22
  52.0 2.9 cholesky.89
  56.3 2.4 custom-call.9
  59.7 0.8 copy.122
  60.5 5.4 all-to-all-start
  67.3 7.6 %all-to-all-done = f32[16,32,128]{2,1,0:T(8,128)S(1)} async-done(((f32[16,32,128]{2,1,0:T(8,128)}), f32[16,32,128]{2,1,0:T(8,128)S(1)}, u32[]{:S(2)}, u32[]{:S(2)}) %all-to-all-start) | async-done | bytes 262176 | tf_op jit(solution)/shard_map/all_to_all | solution.py:32
  75.0 1.4 gather_fusion
  76.4 5.2 fusion.9
  81.6 0.7 fusion.43
  82.4 0.8 copy.198
  83.5 5.5 reduce-scatter.3.cloned.1.call-done
  89.0 1.2 fusion.143
  90.2 40.5 %psum.78 = f32[32,32]{0,1:T(8,128)S(1)} all-reduce(f32[32,32]{0,1:T(8,128)S(1)} %fusion.143), channel_id=1, replica_groups=mesh['row'=16,'col'=2] {'row','col'}, use_global_device_ids=true, to_apply=%region_6.9 | all-reduce | flops 1024 | bytes 8192 | tf_op jit(solution)/shard_map/psum | solution.py:103
  130.8 2.9 cholesky.100
  134.4 0.8 multiply_reduce_fusion.1
  135.2 2.4 custom-call.10
  137.6 1.2 fusion.69
  138.9 2.2 all_gather.6
  141.1 1.4 gather_fusion.1
  142.5 3.5 fusion.12
  146.0 0.7 fusion.41
  146.7 0.8 copy.128
  147.5 5.4 all-to-all-start.1
  153.0 1.0 convolution_bitcast_fusion
  155.4 108.3 %all-reduce.3.cloned.1.call-done = f32[16384]{0:T(1024)} async-done(((f32[16384]{0:T(1024)}), f32[16384]{0:T(1024)}) %all-reduce.3.cloned.1.call-update) | async-done | bytes 65552
  263.7 1.3 fusion.140
  265.0 39.7 %pmax.7 = f32[]{:T(128)} all-reduce(f32[]{:T(128)} %get-tuple-element.23), channel_id=1, replica_groups=mesh['row'=16,'col'=2] {'row','col'}, use_global_device_ids=true, to_apply=%region_11.14 | all-reduce | flops 1 | bytes 8 | tf_op jit(solution)/shard_map/pmax | solution.py:89
  305.7 1.0 convolution_subtract_fusion.7
  307.0 39.9 %psum.79 = f32[32,32]{0,1:T(8,128)S(1)} all-reduce(f32[32,32]{0,1:T(8,128)S(1)} %fusion.49), channel_id=1, replica_groups=mesh['row'=16,'col'=2] {'row','col'}, use_global_device_ids=true, to_apply=%region_12.15 | all-reduce | flops 1024 | bytes 8192 | tf_op jit(solution)/shard_map/psum | solution.py:113
  347.5 40.4 %psum.80 = f32[32,32]{0,1:T(8,128)S(1)} all-reduce(f32[32,32]{0,1:T(8,128)S(1)} %fusion.144), channel_id=1, replica_groups=mesh['row'=16,'col'=2] {'row','col'}, use_global_device_ids=true, to_apply=%region_13.16 | all-reduce | flops 1024 | bytes 8192 | tf_op jit(solution)/shard_map/psum | solution.py:113
  388.4 39.8 %psum.81 = f32[32,32]{0,1:T(8,128)S(1)} all-reduce(f32[32,32]{0,1:T(8,128)S(1)} %fusion.145), channel_id=1, replica_groups=mesh['row'=16,'col'=2] {'row','col'}, use_global_device_ids=true, to_apply=%region_14.17 | all-reduce | flops 1024 | bytes 8192 | tf_op jit(solution)/shard_map/psum | solution.py:113
  428.8 40.3 %psum.82 = f32[32,32]{0,1:T(8,128)S(1)} all-reduce(f32[32,32]{0,1:T(8,128)S(1)} %fusion.146), channel_id=1, replica_groups=mesh['row'=16,'col'=2] {'row','col'}, use_global_device_ids=true, to_apply=%region_15.18 | all-reduce | flops 1024 | bytes 8192 | tf_op jit(solution)/shard_map/psum | solution.py:22
  469.2 2.9 cholesky.111
  473.4 2.4 custom-call.11
  476.6 13.9 %all_to_all.20 = f32[16,32,128]{2,1,0:T(8,128)S(1)} all-to-all(f32[16,32,128]{2,1,0:T(8,128)S(1)} %copy.137), channel_id=1, replica_groups=mesh['row'=16,'col'=2] {'row'}, dimensions={0} | all-to-all | bytes 524288 | tf_op jit(solution)/shard_map/all_to_all | solution.py:32
  490.5 1.4 gather_fusion.2
  491.9 5.2 fusion.15
  497.2 0.7 fusion.39
  497.9 0.8 copy.197
  498.7 5.8 reduce-scatter.5.cloned.1.call-done
  504.5 1.2 fusion.147
  505.8 40.5 %psum.83 = f32[32,32]{0,1:T(8,128)S(1)} all-reduce(f32[32,32]{0,1:T(8,128)S(1)} %fusion.147), channel_id=1, replica_groups=mesh['row'=16,'col'=2] {'row','col'}, use_global_device_ids=true, to_apply=%region_17.20 | all-reduce | flops 1024 | bytes 8192 | tf_op jit(solution)/shard_map/psum | solution.py:103
  546.4 2.9 cholesky.122
  550.0 0.7 fusion.120
  550.7 2.4 custom-call.12
  553.2 1.2 fusion.63
  554.4 2.0 all_gather.7
  556.4 1.4 gather_fusion.3
  557.9 3.4 fusion.18
  561.3 0.7 fusion.37
  562.0 0.8 copy.143
  562.8 5.4 all-to-all-start.3
  568.3 0.7 copy.151
  569.6 8.8 %all-to-all-done.3 = f32[16,32,128]{2,1,0:T(8,128)S(1)} async-done(((f32[16,32,128]{2,1,0:T(8,128)}), f32[16,32,128]{2,1,0:T(8,128)S(1)}, u32[]{:S(2)}, u32[]{:S(2)}) %all-to-all-start.3) | async-done | bytes 262176 | tf_op jit(solution)/shard_map/all_to_all | solution.py:51
  578.8 0.9 convolution_subtract_fusion.3
  580.1 38.9 %psum.84 = f32[32,32]{0,1:T(8,128)S(1)} all-reduce(f32[32,32]{0,1:T(8,128)S(1)} %fusion.50), channel_id=1, replica_groups=mesh['row'=16,'col'=2] {'row','col'}, use_global_device_ids=true, to_apply=%region_19.22 | all-reduce | flops 1024 | bytes 8192 | tf_op jit(solution)/shard_map/psum | solution.py:113
  619.5 39.9 %psum.85 = f32[32,32]{0,1:T(8,128)S(1)} all-reduce(f32[32,32]{0,1:T(8,128)S(1)} %fusion.148), channel_id=1, replica_groups=mesh['row'=16,'col'=2] {'row','col'}, use_global_device_ids=true, to_apply=%region_20.23 | all-reduce | flops 1024 | bytes 8192 | tf_op jit(solution)/shard_map/psum | solution.py:113
  659.9 40.5 %psum.86 = f32[32,32]{0,1:T(8,128)S(1)} all-reduce(f32[32,32]{0,1:T(8,128)S(1)} %fusion.149), channel_id=1, replica_groups=mesh['row'=16,'col'=2] {'row','col'}, use_global_device_ids=true, to_apply=%region_21.24 | all-reduce | flops 1024 | bytes 8192 | tf_op jit(solution)/shard_map/psum | solution.py:113
  700.9 39.9 %psum.87 = f32[32,32]{0,1:T(8,128)S(1)} all-reduce(f32[32,32]{0,1:T(8,128)S(1)} %fusion.150), channel_id=1, replica_groups=mesh['row'=16,'col'=2] {'row','col'}, use_global_device_ids=true, to_apply=%region_22.25 | all-reduce | flops 1024 | bytes 8192 | tf_op jit(solution)/shard_map/psum | solution.py:22
  740.9 2.9 cholesky.133
  745.1 2.4 custom-call.13
  747.6 1.0 fusion.60
  (84 shorter events, 16.0 us)
Async XLA Ops:
  8.0 1.6 copy-start
  8.0 68.4 %copy-start.1 = (f32[1,1,40,128,128]{4,3,2,1,0:T(8,128)S(1)}, f32[1,1,40,128,128]{4,3,2,1,0:T(8,128)}, u32[]{:S(2)}) copy-start(f32[1,1,40,128,128]{4,3,2,1,0:T(8,128)} %param.8) | copy-start | bytes 7864324
  60.5 14.5 %all-to-all-start = ((f32[16,32,128]{2,1,0:T(8,128)}), f32[16,32,128]{2,1,0:T(8,128)S(1)}, u32[]{:S(2)}, u32[]{:S(2)}) async-start(f32[16,32,128]{2,1,0:T(8,128)} %copy.122), calls=%async_computation | async-start | bytes 524288 | tf_op jit(solution)/shard_map/all_to_all | solution.py:32
  65.9 23.1 %reduce-scatter.3.cloned.1.call-start = ((), (), s32[]{:S(2)}) async-start(), calls=%async_computation.6 | async-start | bytes 393216 | tf_op jit(solution)/shard_map/reduce_scatter | solution.py:38
  67.3 14.3 %copy-start.3 = (s32[1,1,40]{2,1,0:T(1,128)S(1)}, s32[1,1,40]{2,1,0:T(1,128)}, u32[]{:S(2)}) copy-start(s32[1,1,40]{2,1,0:T(1,128)} %param.9) | copy-start | bytes 484
  142.5 11.5 %copy-start.5 = (u32[32]{0:T(128)S(1)}, u32[32]{0:T(128)}, u32[]{:S(2)}) copy-start(u32[32]{0:T(128)} %constant.104) | copy-start | bytes 388
  142.5 12.7 %copy-start.4 = (s32[16]{0:T(128)S(1)}, s32[16]{0:T(128)}, u32[]{:S(2)}) copy-start(s32[16]{0:T(128)} %param.12) | copy-start | bytes 196
  147.5 157.9 %all-to-all-start.1 = ((f32[16,32,128]{2,1,0:T(8,128)}), f32[16,32,128]{2,1,0:T(8,128)S(1)}, u32[]{:S(2)}, u32[]{:S(2)}) async-start(f32[16,32,128]{2,1,0:T(8,128)} %copy.128), calls=%async_computation.2 | async-start | bytes 524288 | tf_op jit(solution)/shard_map/all_to_all | solution.py:51
  152.9 110.8 %all-reduce.3.cloned.1.call-start = ((), (), s32[]{:S(2)}) async-start(), calls=%async_computation.8 | async-start | bytes 131072
  154.0 350.6 %reduce-scatter.5.cloned.1.call-start = ((), (), s32[]{:S(2)}) async-start(), calls=%async_computation.7 | async-start | bytes 393216 | tf_op jit(solution)/shard_map/reduce_scatter | solution.py:38
  554.4 6.9 copy-start.2
  562.8 15.6 %all-to-all-start.3 = ((f32[16,32,128]{2,1,0:T(8,128)}), f32[16,32,128]{2,1,0:T(8,128)S(1)}, u32[]{:S(2)}, u32[]{:S(2)}) async-start(f32[16,32,128]{2,1,0:T(8,128)} %copy.143), calls=%async_computation.5 | async-start | bytes 524288 | tf_op jit(solution)/shard_map/all_to_all | solution.py:51
Sparse Core Ops, SparseCore 0:
  83.3 5.6 reduce-scatter.2
  498.8 5.6 reduce-scatter.4
Sparse Core Ops, SparseCore 1:
  159.5 104.2 all-reduce.2
where the time goes:
time: 759 us; the launch traced here: 756 us
  blocking collectives  501 us (66%)
  waiting for transfers between devices  136 us (18%)
  other arithmetic  39.9 us (5%)
  matrix products  34.9 us (5%)
  between operations  16.6 us (2%)
  starting transfers between devices  16.5 us (2%)
  local copies, waits for them, and re-layouts  11.4 us (2%)
    psum x6, blocking collectives, shards(): lax.psum(jnp.dot(right_now, (squares[None, :] * correction).T, precision=...  239 us
    psum x3, blocking collectives, basis_factor(): gram_sum = lax.psum(gram_local(trial_basis), ('row', 'col'))  122 us
    unnamed x4, waiting for transfers between devices  108 us
    psum x2, blocking collectives, shards(): gram_image = lax.psum(gram_local(image_own), ('row', 'col'))  81 us
    pmax x1, blocking collectives, shards(): largest = lax.pmax(jnp.max(squares), ('row', 'col'))  39.7 us
  transfers between devices with their start and end apart: 6, of which 5 were waited for; matrix products, arithmetic and copies ran while one was open for 1% of the time, Pallas kernels for 0%

commit v1 on v0

v1 whole, which is shorter than its diff:
```python
import functools

import jax
import jax.numpy as jnp
from jax import lax
from jax.experimental import pallas as pl
from jax.experimental.pallas import tpu as pltpu
from jax.sharding import PartitionSpec as P

OUTER = 2
INNER = 4
PAD = 8

highest = lax.Precision.HIGHEST
f32 = jnp.float32


def mm(a, b):
    return lax.dot_general(a, b, (((1,), (0,)), ((), ())), precision=highest, preferred_element_type=f32)


def mt(a, b):
    return lax.dot_general(a, b, (((1,), (1,)), ((), ())), precision=highest, preferred_element_type=f32)


def lanes(values):
    return jnp.concatenate(values, axis=1)


def column(row):
    count = row.shape[1]
    eye = lax.broadcasted_iota(jnp.int32, (count, count), 0) == lax.broadcasted_iota(
        jnp.int32, (count, count), 1
    )
    return jnp.sum(jnp.where(eye, row, 0.0), axis=1, keepdims=True)


def axis_parts(x, axis):
    count = lax.axis_size(axis)
    if count & (count - 1):
        return [lax.psum(x, axis)]
    parts = [x]
    bit = 1
    while bit < count:
        if len(parts) > 1:
            x = functools.reduce(jnp.add, parts)
        masks = (bit, 2 * bit, 3 * bit) if 2 * bit < count else (bit,)
        parts = [x] + [
            lax.ppermute(x, axis, [(i, i ^ mask) for i in range(count)]) for mask in masks
        ]
        bit *= 4
    return parts


def axis_sum(x, axis):
    return functools.reduce(jnp.add, axis_parts(x, axis))


def exchange(x):
    return lax.all_to_all(x, "row", split_axis=0, concat_axis=0, tiled=True)


smem = pl.BlockSpec(memory_space=pltpu.SMEM)
vmem = pl.BlockSpec(memory_space=pltpu.VMEM)


def call(kernel, outs, args, scratch=(), name=None):
    specs = [smem if jnp.issubdtype(a.dtype, jnp.integer) else vmem for a in args]
    return pl.pallas_call(
        kernel,
        out_shape=tuple(jax.ShapeDtypeStruct(s, f32) for s in outs),
        in_specs=specs,
        out_specs=tuple(vmem for _ in outs),
        scratch_shapes=list(scratch),
        compiler_params=pltpu.CompilerParams(vmem_limit_bytes=32 << 20),
        name=name,
    )(*args)


def seg_slice(index, size):
    return pl.ds(pl.multiple_of(index * size, size), size)


def factor_inverse(gram_sum):
    count = gram_sum.shape[0]
    rows = lax.broadcasted_iota(jnp.int32, (count, count), 0)
    cols = lax.broadcasted_iota(jnp.int32, (count, count), 1)
    state = lanes([gram_sum, jnp.where(rows == cols, 1.0, 0.0)])
    below = lax.broadcasted_iota(jnp.int32, (count, 1), 0)
    for k in range(count):
        pivot_row = state[k : k + 1, :]
        scaled = pivot_row / state[k : k + 1, k : k + 1]
        factor = jnp.where(below > k, state[:, k : k + 1], 0.0)
        state = state - factor * scaled
    left = state[:, :count]
    diag = jnp.sum(jnp.where(rows == cols, left, 0.0), axis=1, keepdims=True)
    state = state * (1.0 / jnp.sqrt(diag))
    return jnp.where(cols >= rows, state[:, :count], 0.0), state[:, count:]


def factor(gram_v, gram_y, top, total_rows):
    unused, lower_inv = factor_inverse(gram_v / total_rows)
    gram_image = mt(mm(lower_inv, gram_y / total_rows), lower_inv)
    upper, image_inv = factor_inverse(gram_image)
    sums = jnp.sum(upper * upper, axis=0, keepdims=True)
    scale = column(top / (sums + top))
    return lower_inv, upper, mm(image_inv, lower_inv), scale


def couple(facts, moments_vv, moments_wv, total_rows):
    lower_inv, upper, to_left, scale = facts
    bb = [mt(mm(lower_inv, m / total_rows), lower_inv) for m in moments_vv]
    rb = [
        mt(mm(to_left, m / total_rows), lower_inv) - mm(upper, b)
        for m, b in zip(moments_wv, bb)
    ]
    powers = [scale]
    for _ in range(INNER - 2):
        powers.append(powers[-1] * scale)
    couplings = []
    base = 0.0
    for m in range(INNER - 1):
        base = base + powers[m] * rb[m]
        value = base
        for k in range(m):
            value = value - powers[k] * mm(couplings[m - 1 - k], bb[k])
        couplings.append(value)
    on_basis = [lower_inv, -mm(upper, lower_inv)] + [mm(c, lower_inv) for c in couplings]
    return jnp.concatenate(on_basis, axis=0)


def correct(on_basis, to_left, scale, gain, cols_v, cols_w, cols_s):
    count = to_left.shape[0]
    mixed = mm(on_basis, cols_v)
    part = lambda k: mixed[k * count : (k + 1) * count]
    basis = part(0)
    residual = part(1) + mm(to_left, cols_w)
    correction = scale * residual
    for m in range(INNER - 1):
        correction = scale * (residual + cols_s * correction - part(2 + m))
    return basis + gain * correction


def selected(targets, count):
    rows = lax.broadcasted_iota(jnp.int32, (count, 1), 0)
    chosen = jnp.zeros((count, 1), f32)
    for t in range(targets.shape[0]):
        chosen = chosen + jnp.where(rows == targets[t], 1.0, 0.0)
    return chosen


def apply_tiles(tiles, rows, owners, source, image, size):
    count = tiles.shape[0]
    image[...] = jnp.zeros_like(image)

    def step(n, carry):
        at = seg_slice(rows[n], size)
        image[:, at] += mt(source(owners[n]), tiles[n])
        return carry

    lax.fori_loop(0, count, step, 0, unroll=8)


def apply_back(tiles, rows, owners, image, send, vectors, size):
    count = tiles.shape[0]

    def step(n, carry):
        picked = image[:vectors, seg_slice(rows[n], size)]
        send[owners[n], :vectors, :] += mm(picked, tiles[n])
        return carry

    lax.fori_loop(0, count, step, 0, unroll=8)


def pack_kernel(tiles, vectors, segs, owners, send):
    size = tiles.shape[-1]
    count = vectors.shape[0]
    send[:, count:, :] = jnp.zeros((send.shape[0], PAD, size), f32)
    for r in range(send.shape[0]):
        send[r, :count, :] = vectors[:, seg_slice(segs[r], size)]

    def step(n, carry):
        tile = tiles[n]
        send[owners[n], count : count + 1, :] += jnp.sum(tile * tile, axis=0, keepdims=True)
        return carry

    lax.fori_loop(0, tiles.shape[0], step, 0, unroll=8)


def first_kernel(slot, tiles, got, vectors, segs, rows, owners, image, squares):
    size = tiles.shape[-1]
    count = vectors.shape[0]
    span = image.shape[1] - size
    squares[...] = jnp.zeros_like(squares)
    for r in range(got.shape[0]):
        squares[:, seg_slice(segs[r], size)] += got[r, count : count + PAD, :]
    apply_tiles(tiles, rows, owners, lambda o: got[o, :count, :], image, size)
    image[:, span:] = jnp.zeros((count, size), f32)
    image[:, span : span + count] = mt(vectors[...], vectors[...])
    where = lax.broadcasted_iota(jnp.int32, (count, size - count), 1) == slot[0]
    image[:, span + count :] = jnp.where(where, jnp.max(squares[...]), 0.0)


def first_back_kernel(parts_count, tiles, rows, owners, *refs):
    parts, send, image = refs[:parts_count], refs[-2], refs[-1]
    size = tiles.shape[-1]
    count = image.shape[0]
    span = image.shape[1] - size
    image[...] = functools.reduce(jnp.add, [p[...] for p in parts])
    top = jnp.max(image[:, span + count :])
    summed = image[:, :span]
    gram_y = mt(summed, summed)
    gram_v = image[:, span : span + count]
    half = count // 2
    extra = lanes(
        [gram_v[:half], gram_v[half:], gram_y[:half], gram_y[half:]]
    )
    send[:, :count, :] = jnp.zeros((send.shape[0], count, size), f32)
    for r in range(send.shape[0]):
        send[r, count : count + half, :] = extra
        send[r, count + half :, :] = jnp.broadcast_to(top, (PAD, size))
    apply_back(tiles, rows, owners, image, send, count, size)


def powers_of(values, scales):
    powers = [values]
    for _ in range(INNER - 1):
        powers.append(powers[-1] * scales)
    return powers


def gather_cols(got, segs, cols, count, size):
    cols[...] = jnp.zeros_like(cols)
    for r in range(got.shape[0]):
        cols[:, seg_slice(segs[r], size)] += got[r, :count, :]


def moment_kernel(got, vectors, squares, segs, send, moments, small, own_w, own_s):
    count = vectors.shape[0]
    size = got.shape[-1]
    half = count // 2
    gather_cols(got, segs, own_w, count, size)
    extra = got[0, count : count + half, :]
    top = got[0, count + half :, :]
    for r in range(1, got.shape[0]):
        extra = extra + got[r, count : count + half, :]
        top = jnp.maximum(top, got[r, count + half :, :])
    largest = jnp.max(top)
    own_s[...] = squares[...] / largest
    small[...] = jnp.zeros_like(small)
    small[:half, :count] = extra[:, :count]
    small[half:, :count] = extra[:, count : 2 * count]
    small[:half, count : 2 * count] = extra[:, 2 * count : 3 * count]
    small[half:, count : 2 * count] = extra[:, 3 * count : 4 * count]
    small[:, 2 * count :] = jnp.broadcast_to(largest, (count, size - 2 * count))
    for r in range(send.shape[0]):
        at = seg_slice(segs[r], size)
        send[r, :count, :] = own_w[:, at]
        send[r, count:, :] = own_s[:, at]
    values = vectors[...]
    both = jnp.concatenate([values, own_w[...]], axis=0)
    scales = own_s[0:1, :]
    moments[...] = jnp.zeros_like(moments)
    for j in range(1, INNER):
        values = values * scales
        found = mt(both, values)
        moments[:, (j - 1) * count : j * count] = found[:count]
        moments[:, size + (j - 1) * count : size + j * count] = found[count:]


def factor_kernel(total_rows, small, facts):
    count = small.shape[0]
    lower_inv, upper, to_left, scale = factor(
        small[:, :count],
        small[:, count : 2 * count],
        small[0:1, 2 * count : 2 * count + 1],
        total_rows,
    )
    facts[0] = lower_inv
    facts[1] = upper
    facts[2] = to_left
    facts[3] = jnp.broadcast_to(scale, (count, count))


def second_kernel(
    total_rows, parts_count, tiles, got_v, got, vectors, own_w, own_s, small, facts,
    targets, rows, owners, *refs
):
    parts = refs[:parts_count]
    image, own_next, powers = refs[parts_count:]
    count = vectors.shape[0]
    size = tiles.shape[-1]
    span = image.shape[1] - size
    moments = functools.reduce(jnp.add, [p[...] for p in parts])
    moments_vv = [moments[:, k * count : (k + 1) * count] for k in range(INNER - 1)]
    moments_wv = [moments[:, size + k * count : size + (k + 1) * count] for k in range(INNER - 1)]
    to_left, scale = facts[2], facts[3][:, 0:1]
    on_basis = couple((facts[0], facts[1], to_left, scale), moments_vv, moments_wv, total_rows)
    gain = selected(targets, count) / small[:, 2 * count : 2 * count + 1]
    tile_v = lanes([got_v[r, :count, :] for r in range(got.shape[0])])
    tile_w = lanes([got[r, :count, :] for r in range(got.shape[0])])
    tile_s = lanes([got[r, count : count + 1, :] for r in range(got.shape[0])])
    tile_v = correct(on_basis, to_left, scale, gain, tile_v, tile_w, tile_s)
    for k in range(INNER):
        for r in range(got.shape[0]):
            powers[r, k * count : (k + 1) * count, :] = tile_v[:, r * size : (r + 1) * size]
        if k + 1 < INNER:
            tile_v = tile_v * tile_s
    own = correct(on_basis, to_left, scale, gain, vectors[...], own_w[...], own_s[0:1, :])
    own_next[...] = own
    apply_tiles(tiles, rows, owners, lambda o: powers[o], image, size)
    image[count:, span:] = jnp.zeros((image.shape[0] - count, size), f32)
    values = own
    for k in range(INNER):
        image[:count, span + k * count : span + (k + 1) * count] = mt(own, values)
        values = values * own_s[0:1, :]


def second_back_kernel(parts_count, tiles, rows, owners, *refs):
    parts, (send, moments, image) = refs[:parts_count], refs[parts_count:]
    size = tiles.shape[-1]
    count = image.shape[0]
    span = image.shape[1]
    image[...] = functools.reduce(jnp.add, [p[:count, :span] for p in parts])
    moments[:, :size] = functools.reduce(jnp.add, [p[:count, span:] for p in parts])
    summed = image[...]
    others = functools.reduce(jnp.add, [p[:, :span] for p in parts])
    found = mt(summed, others)
    moments[:, size:] = found
    send[...] = jnp.zeros_like(send)
    apply_back(tiles, rows, owners, image, send, count, size)


def second_factor_kernel(total_rows, parts_count, small, *refs):
    parts, (facts, on_basis) = refs[:parts_count], refs[parts_count:]
    count = small.shape[0]
    size = small.shape[1]
    moments = functools.reduce(jnp.add, [p[...] for p in parts])
    pick = lambda k: moments[:, k * count : (k + 1) * count]
    found = factor(pick(0), pick(INNER), small[0:1, 2 * count : 2 * count + 1], total_rows)
    facts[0] = found[0]
    facts[1] = found[1]
    facts[2] = found[2]
    facts[3] = jnp.broadcast_to(found[3], (count, count))
    on_basis[...] = couple(
        found,
        [pick(k) for k in range(1, INNER)],
        [pick(INNER + k) for k in range(1, INNER)],
        total_rows,
    )


def trial_kernel(got, vectors, own_s, small, facts, on_basis, segs, targets, trial, gram_part, own_w):
    count = vectors.shape[0]
    size = got.shape[-1]
    gather_cols(got, segs, own_w, count, size)
    gain = selected(targets, count) / small[:, 2 * count : 2 * count + 1]
    found = correct(
        on_basis[...], facts[2], facts[3][:, 0:1], gain, vectors[...], own_w[...], own_s[0:1, :]
    )
    trial[...] = found
    gram_sum = mt(found, found)
    rows = gram_part.shape[0]
    gram_part[...] = lanes([gram_sum[k * rows : (k + 1) * rows] for k in range(count // rows)])


def last_kernel(total_rows, got, trial, image, facts, right, left):
    count = trial.shape[0]
    packed = got[0]
    for r in range(1, got.shape[0]):
        packed = packed + got[r]
    gram_sum = jnp.concatenate(
        [packed[:, k * count : (k + 1) * count] for k in range(packed.shape[1] // count)], axis=0
    )
    left[...] = mm(facts[2], image[...])
    unused, lower_inv = factor_inverse(gram_sum / total_rows)
    right[...] = mm(lower_inv, trial[...])


def shards(blocks, block_rows, block_cols, start_basis, targets):
    size = blocks.shape[-1]
    tiles = blocks.reshape(-1, size, size)
    rows = block_rows.reshape(-1)
    row_count = lax.axis_size("row")
    col_count = lax.axis_size("col")
    count, width = start_basis.shape
    seg_count = width // size
    span = col_count * width
    total_rows = float(width * row_count * col_count)
    pattern = block_cols[:, 0, :]
    me_row = lax.axis_index("row")
    me_col = lax.axis_index("col")
    owners = lax.dynamic_index_in_dim(pattern, me_row, 0, keepdims=False) // seg_count
    segs = jnp.max(
        jnp.where(pattern // seg_count == me_row, pattern % seg_count, 0), axis=1
    )
    slot = me_col.reshape(1)

    (send,) = call(
        pack_kernel, [(row_count, count + PAD, size)], [tiles, start_basis, segs, owners], name="pack"
    )
    got_v = exchange(send)
    part, squares = call(
        first_kernel,
        [(count, span + size), (PAD, width)],
        [slot, tiles, got_v, start_basis, segs, rows, owners],
        name="first",
    )
    parts = axis_parts(part, "col")
    (send,) = call(
        functools.partial(first_back_kernel, len(parts)),
        [(row_count, count + count // 2 + PAD, size)],
        [tiles, rows, owners] + parts,
        scratch=[pltpu.VMEM((count, span + size), f32)],
        name="first_back",
    )
    got = exchange(send)
    send, moments, small, own_w, own_s = call(
        moment_kernel,
        [
            (row_count, count + PAD, size),
            (count, 2 * size),
            (count, size),
            (count, width),
            (PAD, width),
        ],
        [got, start_basis, squares, segs],
        name="moments",
    )
    got = exchange(send)
    parts = axis_parts(axis_sum(moments, "col"), "row")
    (facts,) = call(
        functools.partial(factor_kernel, total_rows), [(4, count, count)], [small], name="factor"
    )
    part, own_v = call(
        functools.partial(second_kernel, total_rows, len(parts)),
        [(INNER * count, span + size), (count, width)],
        [tiles, got_v, got, start_basis, own_w, own_s, small, facts, targets, rows, owners] + parts,
        scratch=[pltpu.VMEM((row_count, INNER * count, size), f32)],
        name="second",
    )
    parts = axis_parts(part, "col")
    send, moments, image = call(
        functools.partial(second_back_kernel, len(parts)),
        [(row_count, count, size), (count, 2 * size), (count, span)],
        [tiles, rows, owners] + parts,
        name="second_back",
    )
    got = exchange(send)
    parts = axis_parts(moments, "row")
    facts, on_basis = call(
        functools.partial(second_factor_kernel, total_rows, len(parts)),
        [(4, count, count), ((INNER + 1) * count, count)],
        [small] + parts,
        name="second_factor",
    )
    trial, gram_part = call(
        trial_kernel,
        [(count, width), (count * count // size, size)],
        [got, own_v, own_s, small, facts, on_basis, segs, targets],
        scratch=[pltpu.VMEM((count, width), f32)],
        name="trial",
    )
    gram_part = axis_sum(gram_part, "col")
    got = exchange(jnp.broadcast_to(gram_part[None], (row_count,) + gram_part.shape))
    image_own = lax.dynamic_slice_in_dim(image, me_col * width, width, axis=1)
    right, left = call(
        functools.partial(last_kernel, total_rows),
        [(count, width), (count, width)],
        [got, trial, image_own, facts],
        name="last",
    )
    return right, left, facts[1]


def solution(mesh):
    in_specs = (
        P("row", "col", None, None, None),
        P("row", "col", None),
        P(None, "col", None),
        P(None, ("row", "col")),
        P(),
    )
    out_specs = (P(None, ("row", "col")), P(None, ("row", "col")), P())
    return jax.shard_map(shards, mesh=mesh, in_specs=in_specs, out_specs=out_specs, check_vma=False)
```

time: 759 us -> 155 us (0.20)
  blocking collectives: 501 us -> 17.5 us
  waiting for transfers between devices: 136 us -> 36.9 us
  Pallas kernels: 0 us -> 46.6 us
  other arithmetic: 39.9 us -> 1.52 us
  matrix products: 34.9 us -> 0 us
  starting transfers between devices: 16.5 us -> 37.8 us
  between operations: 16.6 us -> 0.82 us
    psum x11 -> x0, blocking collectives: 443 us -> none  [the longest x6 239 us: shards(): lax.psum(jnp.dot(right_now, (squares[None, :] * correction).T, precision=...]
    unnamed x4 -> x0, waiting for transfers between devices: 108 us -> none
    pallas_call x0 -> x10, Pallas kernels: none -> 46.6 us  [call(): pl.pallas_call(kernel, out_shape=tuple((jax.ShapeDtypeStruct(s, f32) for...]
    pmax x1 -> x0, blocking collectives: 39.7 us -> none  [shards(): largest = lax.pmax(jnp.max(squares), ('row', 'col'))]
    another operation x23 -> x0, other arithmetic: 32.1 us -> none  [the longest x8 14.1 us: lower_solve(): lax.linalg.triangular_solve(lower, vectors, left_side=True, lower=True)]
    dot_general x32 -> x0, matrix products: 30.7 us -> none  [the longest x2 10.5 us: multiply(): jnp.einsum('nij,nkj->kni', block_tiles, picked, precision=highest)]
    ppermute x0 -> x16, waiting for transfers between devices: none -> 18.7 us  [axis_parts(): lax.ppermute(x, axis, [(i, i ^ mask) for i in range(count)])]
    ppermute x0 -> x16, starting transfers between devices: none -> 16.1 us  [axis_parts(): lax.ppermute(x, axis, [(i, i ^ mask) for i in range(count)])]
  transfers between devices with their start and end apart: 6 -> 20, of which waited for: 5 -> 14; matrix products, arithmetic and copies ran while one was open for 1% -> 0% of each run, Pallas kernels for 0% -> 9%
where the time goes in v1:
time: 155 us; the launch traced here: 154 us
  Pallas kernels  46.6 us (30%)
  starting transfers between devices  37.8 us (24%)
  waiting for transfers between devices  36.9 us (24%)
  blocking collectives  17.5 us (11%)
  local copies, waits for them, and re-layouts  13 us (8%)
    pallas_call x10, Pallas kernels, call(): pl.pallas_call(kernel, out_shape=tuple((jax.ShapeDtypeStruct(s, f32) for...  46.6 us
    all_to_all x4, starting transfers between devices, exchange(): return lax.all_to_all(x, 'row', split_axis=0, concat_axis=0, tiled=True)  21.7 us
    ppermute x16, waiting for transfers between devices, axis_parts(): lax.ppermute(x, axis, [(i, i ^ mask) for i in range(count)])  18.7 us
    all_to_all x4, waiting for transfers between devices, exchange(): return lax.all_to_all(x, 'row', split_axis=0, concat_axis=0, tiled=True)  18.2 us
    all_to_all x1, blocking collectives, exchange(): return lax.all_to_all(x, 'row', split_axis=0, concat_axis=0, tiled=True)  17.5 us
    ppermute x16, starting transfers between devices, axis_parts(): lax.ppermute(x, axis, [(i, i ^ mask) for i in range(count)])  16.1 us
    unnamed x50, local copies, waits for them, and re-layouts  11.7 us
  transfers between devices with their start and end apart: 20, of which 14 were waited for; matrix products, arithmetic and copies ran while one was open for 0% of the time, Pallas kernels for 9%

profile of v1, /device:TPU:0, one launch (start us, length us, event | category | flops | bytes accessed | tf_op | source)
XLA Modules:
  0.0 154.1 jit_solution(3827189391818857169)
XLA Ops:
  0.6 0.7 and_select_fusion.owners
  1.3 0.8 fusion.2.segs
  2.1 0.0 copy-start
  2.1 1.7 %copy-done = f32[1,1,40,128,128]{4,3,2,1,0:T(8,128)S(1)} copy-done((f32[1,1,40,128,128]{4,3,2,1,0:T(8,128)S(1)}, f32[1,1,40,128,128]{4,3,2,1,0:T(8,128)}, u32[]{:S(2)}) %copy-start) | copy-done | bytes 2621464
  3.9 0.9 copy-done.2
  4.8 1.6 %pack.1 = f32[16,40,128]{2,1,0:T(8,128)} custom-call(f32[40,128,128]{2,1,0:T(8,128)S(1)} %bitcast.14, f32[32,1024]{1,0:T(8,128)S(1)} %copy-done.2, s32[16]{0:T(128)S(1)} %fusion.2.segs, s32[40]{0:T(128)S(1)} %and_select_fusion.owners), custom_call_target="tpu_custom_call" | custom-call | tf_op jit(solution)/shard_map/pack/pallas_call | solution.py:69
  6.4 8.3 %all-to-all-start = ((f32[16,40,128]{2,1,0:T(8,128)}), f32[16,40,128]{2,1,0:T(8,128)S(1)}, u32[]{:S(2)}, u32[]{:S(2)}) async-start(f32[16,40,128]{2,1,0:T(8,128)} %pack.1), calls=%async_computation | async-start | bytes 655360 | tf_op jit(solution)/shard_map/all_to_all | solution.py:60
  14.7 11.3 %all-to-all-done.got.got_v = f32[16,40,128]{2,1,0:T(8,128)S(1)} async-done(((f32[16,40,128]{2,1,0:T(8,128)}), f32[16,40,128]{2,1,0:T(8,128)S(1)}, u32[]{:S(2)}, u32[]{:S(2)}) %all-to-all-start) | async-done | bytes 327712 | tf_op jit(solution)/shard_map/all_to_all | solution.py:60
  26.1 5.5 %first.1 = (f32[32,2176]{1,0:T(8,128)S(1)}, f32[8,1024]{1,0:T(8,128)S(1)}) custom-call(s32[1]{0:T(128)} %bitcast.4.slot, f32[40,128,128]{2,1,0:T(8,128)S(1)} %bitcast.15, f32[16,40,128]{2,1,0:T(8,128)S(1)} %all-to-all-done.got.got_v, f32[32,1024]{1,0:T(8,128)S(1)} %copy-done.3, s32[16]{0:T(128)S(1)} %fusion.2.segs, s32[40]{0:T(128)S(1)} %bitcast.19, ...), custom_call_target="tpu_custom_call" | custom-call | tf_op jit(solution)/shard_map/first/pallas_call | solution.py:69
  31.6 0.1 collective-permute-start
  31.7 1.5 %collective-permute-done.refs_1_ = f32[32,2176]{1,0:T(8,128)S(1)} collective-permute-done((f32[32,2176]{1,0:T(8,128)S(1)}, f32[32,2176]{1,0:T(8,128)S(1)}, u32[]{:S(2)}, u32[]{:S(2)}) %collective-permute-start) | collective-permute-done | bytes 278560 | tf_op jit(solution)/shard_map/ppermute | solution.py:49
  33.2 3.7 %first_back.1 = f32[16,56,128]{2,1,0:T(8,128)S(1)} custom-call(f32[40,128,128]{2,1,0:T(8,128)S(1)} %bitcast.16, s32[40]{0:T(128)S(1)} %bitcast.20, s32[40]{0:T(128)S(1)} %and_select_fusion.owners, f32[32,2176]{1,0:T(8,128)S(1)} %get-tuple-element.21.refs_0_, f32[32,2176]{1,0:T(8,128)S(1)} %collective-permute-done.refs_1_), custom_call_target="tpu_custom_call" | custom-call | tf_op jit(solution)/shard_map/first_back/pallas_call | solution.py:69
  36.9 17.5 %all_to_all.25.got = f32[16,56,128]{2,1,0:T(8,128)S(1)} all-to-all(f32[16,56,128]{2,1,0:T(8,128)S(1)} %first_back.1), channel_id=1, replica_groups=mesh['row'=16,'col'=2] {'row'}, dimensions={0} | all-to-all | bytes 917504 | tf_op jit(solution)/shard_map/all_to_all | solution.py:60
  54.4 1.5 %moments.1 = (f32[16,40,128]{2,1,0:T(8,128)S(1)}, f32[32,256]{1,0:T(8,128)S(1)}, f32[32,128]{1,0:T(8,128)S(1)}, f32[32,1024]{1,0:T(8,128)S(1)}, f32[8,1024]{1,0:T(8,128)S(1)}) custom-call(f32[16,56,128]{2,1,0:T(8,128)S(1)} %all_to_all.25.got, f32[32,1024]{1,0:T(8,128)S(1)} %copy-done.3, f32[8,1024]{1,0:T(8,128)S(1)} %get-tuple-element.22.squares, ...), custom_call_target="tpu_custom_call" | custom-call | tf_op jit(solution)/shard_map/moments/pallas_call | solution.py:69
  55.9 0.7 copy-done.4
  56.6 0.7 copy-done.5
  57.3 3.8 %all-to-all-start.2 = ((f32[16,40,128]{2,1,0:T(8,128)}), f32[16,40,128]{2,1,0:T(8,128)S(1)}, u32[]{:S(2)}, u32[]{:S(2)}) async-start(f32[16,40,128]{2,1,0:T(8,128)} %copy-done.4), calls=%async_computation.2 | async-start | bytes 655360 | tf_op jit(solution)/shard_map/all_to_all | solution.py:60
  61.0 0.1 collective-permute-start.1
  61.1 1.2 collective-permute-done.1
  62.3 2.8 %collective-permute-start.4 = (f32[32,256]{1,0:T(8,128)S(1)}, f32[32,256]{1,0:T(8,128)S(1)}, u32[]{:S(2)}, u32[]{:S(2)}) collective-permute-start(f32[32,256]{1,0:T(8,128)S(1)} %add.41), channel_id=1, source_target_pairs={{0,6},{2,4},{4,2},{6,0},{8,14},{10,12},{12,10},{14,8},{16,22},{18,... | collective-permute-start | bytes 98312 | tf_op jit(solution)/shard_map/ppermute | solution.py:49
  65.1 0.6 collective-permute-start.3
  65.6 0.2 collective-permute-start.2
  65.8 2.5 %collective-permute-done.4 = f32[32,256]{1,0:T(8,128)S(1)} collective-permute-done((f32[32,256]{1,0:T(8,128)S(1)}, f32[32,256]{1,0:T(8,128)S(1)}, u32[]{:S(2)}, u32[]{:S(2)}) %collective-permute-start.4) | collective-permute-done | bytes 32800 | tf_op jit(solution)/shard_map/ppermute | solution.py:49
  68.3 0.7 collective-permute-done.3
  69.0 1.0 collective-permute-done.2
  70.0 3.3 %collective-permute-start.7 = (f32[32,256]{1,0:T(8,128)S(1)}, f32[32,256]{1,0:T(8,128)S(1)}, u32[]{:S(2)}, u32[]{:S(2)}) collective-permute-start(f32[32,256]{1,0:T(8,128)S(1)} %add_add_fusion.1.refs_0_), channel_id=1, source_target_pairs={{0,24},{2,26},{4,28},{6,30},{8,16},{10,18},{12,20},{14,22},{16,8},... | collective-permute-start | bytes 98312 | tf_op jit(solution)/shard_map/ppermute | solution.py:49
  73.3 1.1 collective-permute-start.5
  74.5 6.0 %factor.1.facts = f32[4,32,32]{2,1,0:T(8,128)S(1)} custom-call(f32[32,128]{1,0:T(8,128)S(1)} %get-tuple-element.26.small), custom_call_target="tpu_custom_call" | custom-call | tf_op jit(solution)/shard_map/factor/pallas_call | solution.py:69
  80.5 0.6 copy-done.9
  81.1 0.6 copy-done.11
  81.7 0.6 copy-done.13
  82.4 0.9 copy-done.6
  83.3 0.8 copy-done.10
  84.0 0.8 copy-done.12
  84.8 0.8 copy-done.14
  85.5 0.7 copy-done.18
  86.2 0.7 copy-done.21
  86.9 0.7 copy-done.23
  87.5 10.5 %second.1 = (f32[128,2176]{1,0:T(8,128)S(1)}, f32[32,1024]{1,0:T(8,128)S(1)}) custom-call(f32[40,128,128]{2,1,0:T(8,128)S(1)} %bitcast.17, f32[16,40,128]{2,1,0:T(8,128)S(1)} %all-to-all-done.got.got_v, f32[16,40,128]{2,1,0:T(8,128)S(1)} %all-to-all-done.2.got, f32[32,1024]{1,0:T(8,128)S(1)} %copy-done.3, f32[32,1024]{1,0:T(8,128)S(1)} %copy-done.6, ...), custom_call_target="tpu_custom_call" | custom-call | tf_op jit(solution)/shard_map/second/pallas_call | solution.py:69
  98.0 0.0 copy-start.7
  98.0 0.7 copy-done.7
  98.7 2.7 %collective-permute-done.8.refs_1_ = f32[128,2176]{1,0:T(8,128)S(1)} collective-permute-done((f32[128,2176]{1,0:T(8,128)S(1)}, f32[128,2176]{1,0:T(8,128)S(1)}, u32[]{:S(2)}, u32[]{:S(2)}) %collective-permute-start.8) | collective-permute-done | bytes 1114144 | tf_op jit(solution)/shard_map/ppermute | solution.py:49
  101.4 5.1 %second_back.1 = (f32[16,32,128]{2,1,0:T(8,128)}, f32[32,256]{1,0:T(8,128)S(1)}, f32[32,2048]{1,0:T(8,128)S(1)}) custom-call(f32[40,128,128]{2,1,0:T(8,128)S(1)} %bitcast.18, s32[40]{0:T(128)S(1)} %bitcast.22, s32[40]{0:T(128)S(1)} %copy-done.19, f32[128,2176]{1,0:T(8,128)S(1)} %get-tuple-element.28.refs_0_, f32[128,2176]{1,0:T(8,128)S(1)} %collective-permute-done.8.refs_1_), custom_call_target="tpu_custom_call" | custom-call | tf_op jit(solution)/shard_map/second_back/pallas_call | solution.py:69
  106.5 5.4 %all-to-all-start.3 = ((f32[16,32,128]{2,1,0:T(8,128)}), f32[16,32,128]{2,1,0:T(8,128)S(1)}, u32[]{:S(2)}, u32[]{:S(2)}) async-start(f32[16,32,128]{2,1,0:T(8,128)} %get-tuple-element.29), calls=%async_computation.3 | async-start | bytes 524288 | tf_op jit(solution)/shard_map/all_to_all | solution.py:60
  111.9 2.9 %collective-permute-start.11 = (f32[32,256]{1,0:T(8,128)S(1)}, f32[32,256]{1,0:T(8,128)S(1)}, u32[]{:S(2)}, u32[]{:S(2)}) collective-permute-start(f32[32,256]{1,0:T(8,128)S(1)} %get-tuple-element.31), channel_id=1, source_target_pairs={{0,6},{2,4},{4,2},{6,0},{8,14},{10,12},{12,10},{14,8},{16,22},{18,... | collective-permute-start | bytes 98312 | tf_op jit(solution)/shard_map/ppermute | solution.py:49
  114.8 0.6 collective-permute-start.10
  115.3 0.1 collective-permute-start.9
  115.4 2.1 %collective-permute-done.11 = f32[32,256]{1,0:T(8,128)S(1)} collective-permute-done((f32[32,256]{1,0:T(8,128)S(1)}, f32[32,256]{1,0:T(8,128)S(1)}, u32[]{:S(2)}, u32[]{:S(2)}) %collective-permute-start.11) | collective-permute-done | bytes 32800 | tf_op jit(solution)/shard_map/ppermute | solution.py:49
  117.5 1.3 collective-permute-done.10
  118.8 0.4 collective-permute-done.9
  119.2 3.7 %collective-permute-start.14 = (f32[32,256]{1,0:T(8,128)S(1)}, f32[32,256]{1,0:T(8,128)S(1)}, u32[]{:S(2)}, u32[]{:S(2)}) collective-permute-start(f32[32,256]{1,0:T(8,128)S(1)} %add_add_fusion.refs_0_), channel_id=1, source_target_pairs={{0,24},{2,26},{4,28},{6,30},{8,16},{10,18},{12,20},{14,22},{16,8},... | collective-permute-start | bytes 98312 | tf_op jit(solution)/shard_map/ppermute | solution.py:49
  122.9 0.8 collective-permute-start.12
  123.7 1.3 collective-permute-done.14.refs_3_
  125.0 2.7 %collective-permute-done.13.refs_2_ = f32[32,256]{1,0:T(8,128)S(1)} collective-permute-done((f32[32,256]{1,0:T(8,128)S(1)}, f32[32,256]{1,0:T(8,128)S(1)}, u32[]{:S(2)}, u32[]{:S(2)}) %collective-permute-start.13) | collective-permute-done | bytes 32800 | tf_op jit(solution)/shard_map/ppermute | solution.py:49
  127.7 7.3 %second_factor.1 = (f32[4,32,32]{2,1,0:T(8,128)S(1)}, f32[160,32]{1,0:T(8,128)S(1)}) custom-call(f32[32,128]{1,0:T(8,128)S(1)} %get-tuple-element.26.small, f32[32,256]{1,0:T(8,128)S(1)} %add_add_fusion.refs_0_, f32[32,256]{1,0:T(8,128)S(1)} %collective-permute-done.12.refs_1_, f32[32,256]{1,0:T(8,128)S(1)} %collective-permute-done.13.refs_2_, ...), custom_call_target="tpu_custom_call" | custom-call | tf_op jit(solution)/shard_map/second_factor/pallas_call | solution.py:69
  135.0 0.0 copy-done.16
  135.0 1.7 %trial.1 = (f32[32,1024]{1,0:T(8,128)S(1)}, f32[8,128]{1,0:T(8,128)S(1)}) custom-call(f32[16,32,128]{2,1,0:T(8,128)S(1)} %all-to-all-done.3.got, f32[32,1024]{1,0:T(8,128)S(1)} %copy-done.8, f32[8,1024]{1,0:T(8,128)S(1)} %get-tuple-element.25.own_s, f32[32,128]{1,0:T(8,128)S(1)} %get-tuple-element.26.small, f32[4,32,32]{2,1,0:T(8,128)S(1)} %get-tuple-element.32.facts, ...), custom_call_target="tpu_custom_call" | custom-call | tf_op jit(solution)/shard_map/trial/pallas_call | solution.py:69
  136.7 0.1 collective-permute-start.15
  136.8 1.1 collective-permute-done.15
  137.9 0.6 broadcast_in_dim.4
  138.6 4.2 %all-to-all-start.4 = ((f32[16,8,128]{2,1,0:T(8,128)}), f32[16,8,128]{2,1,0:T(8,128)S(1)}, u32[]{:S(2)}, u32[]{:S(2)}) async-start(f32[16,8,128]{2,1,0:T(8,128)} %broadcast_in_dim.4), calls=%async_computation.4 | async-start | bytes 131072 | tf_op jit(solution)/shard_map/all_to_all | solution.py:60
  142.8 0.6 slice_bitcast_fusion
  143.4 6.9 %all-to-all-done.4.got = f32[16,8,128]{2,1,0:T(8,128)S(1)} async-done(((f32[16,8,128]{2,1,0:T(8,128)}), f32[16,8,128]{2,1,0:T(8,128)S(1)}, u32[]{:S(2)}, u32[]{:S(2)}) %all-to-all-start.4) | async-done | bytes 65568 | tf_op jit(solution)/shard_map/all_to_all | solution.py:60
  150.3 3.7 %last.1 = (f32[32,1024]{1,0:T(8,128)}, f32[32,1024]{1,0:T(8,128)}) custom-call(f32[16,8,128]{2,1,0:T(8,128)S(1)} %all-to-all-done.4.got, f32[32,1024]{1,0:T(8,128)S(1)} %get-tuple-element.35.trial, f32[32,1024]{1,0:T(8,128)S(1)} %constant_dynamic-slice_fusion.image, f32[4,32,32]{2,1,0:T(8,128)S(1)} %get-tuple-element.32.facts), custom_call_target="tpu_custom_call" | custom-call | tf_op jit(solution)/shard_map/last/pallas_call | solution.py:69
  (46 shorter events, 0.1 us)
Async XLA Ops:
  1.3 31.9 %copy-start.17 = (s32[40]{0:T(128)}, s32[40]{0:T(128)S(1)}, u32[]{:S(2)}) copy-start(s32[40]{0:T(128)S(1)} %and_select_fusion.owners) | copy-start | bytes 484
  2.1 52.2 %copy-start.15 = (s32[16]{0:T(128)}, s32[16]{0:T(128)S(1)}, u32[]{:S(2)}) copy-start(s32[16]{0:T(128)S(1)} %fusion.2.segs) | copy-start | bytes 196
  2.1 1.7 %copy-start = (f32[1,1,40,128,128]{4,3,2,1,0:T(8,128)S(1)}, f32[1,1,40,128,128]{4,3,2,1,0:T(8,128)}, u32[]{:S(2)}) copy-start(f32[1,1,40,128,128]{4,3,2,1,0:T(8,128)} %param.5) | copy-start | bytes 7864324
  3.9 0.9 copy-start.2
  4.8 21.3 %copy-start.1 = (f32[1,1,40,128,128]{4,3,2,1,0:T(8,128)S(1)}, f32[1,1,40,128,128]{4,3,2,1,0:T(8,128)}, u32[]{:S(2)}) copy-start(f32[1,1,40,128,128]{4,3,2,1,0:T(8,128)} %param.5) | copy-start | bytes 7864324
  4.8 21.3 %copy-start.3 = (f32[32,1024]{1,0:T(8,128)S(1)}, f32[32,1024]{1,0:T(8,128)}, u32[]{:S(2)}) copy-start(f32[32,1024]{1,0:T(8,128)} %vectors.7) | copy-start | bytes 393220
  4.8 21.3 %copy-start.20 = (s32[1,1,40]{2,1,0:T(1,128)S(1)}, s32[1,1,40]{2,1,0:T(1,128)}, u32[]{:S(2)}) copy-start(s32[1,1,40]{2,1,0:T(1,128)} %param.6) | copy-start | bytes 484
  6.4 19.7 %all-to-all-start = ((f32[16,40,128]{2,1,0:T(8,128)}), f32[16,40,128]{2,1,0:T(8,128)S(1)}, u32[]{:S(2)}, u32[]{:S(2)}) async-start(f32[16,40,128]{2,1,0:T(8,128)} %pack.1), calls=%async_computation | async-start | bytes 655360 | tf_op jit(solution)/shard_map/all_to_all | solution.py:60
  31.6 1.6 %collective-permute-start = (f32[32,2176]{1,0:T(8,128)S(1)}, f32[32,2176]{1,0:T(8,128)S(1)}, u32[]{:S(2)}, u32[]{:S(2)}) collective-permute-start(f32[32,2176]{1,0:T(8,128)S(1)} %get-tuple-element.21.refs_0_), channel_id=1, source_target_pairs={{0,1},{1,0},{2,3},{3,2},{4,5},{5,4},{6,7},{7,6},{8,9},{9,8},{10,11... | collective-permute-start | bytes 835592 | tf_op jit(solution)/shard_map/ppermute | solution.py:49
  55.9 0.7 copy-start.4
  56.6 0.7 copy-start.5
  57.3 25.1 %all-to-all-start.2 = ((f32[16,40,128]{2,1,0:T(8,128)}), f32[16,40,128]{2,1,0:T(8,128)S(1)}, u32[]{:S(2)}, u32[]{:S(2)}) async-start(f32[16,40,128]{2,1,0:T(8,128)} %copy-done.4), calls=%async_computation.2 | async-start | bytes 655360 | tf_op jit(solution)/shard_map/all_to_all | solution.py:60
  61.0 1.3 collective-permute-start.1
  62.3 6.0 %collective-permute-start.4 = (f32[32,256]{1,0:T(8,128)S(1)}, f32[32,256]{1,0:T(8,128)S(1)}, u32[]{:S(2)}, u32[]{:S(2)}) collective-permute-start(f32[32,256]{1,0:T(8,128)S(1)} %add.41), channel_id=1, source_target_pairs={{0,6},{2,4},{4,2},{6,0},{8,14},{10,12},{12,10},{14,8},{16,22},{18,... | collective-permute-start | bytes 98312 | tf_op jit(solution)/shard_map/ppermute | solution.py:49
  65.1 3.9 %collective-permute-start.3 = (f32[32,256]{1,0:T(8,128)S(1)}, f32[32,256]{1,0:T(8,128)S(1)}, u32[]{:S(2)}, u32[]{:S(2)}) collective-permute-start(f32[32,256]{1,0:T(8,128)S(1)} %add.41), channel_id=1, source_target_pairs={{0,4},{2,6},{4,0},{6,2},{8,12},{10,14},{12,8},{14,10},{16,20},{18,... | collective-permute-start | bytes 98312 | tf_op jit(solution)/shard_map/ppermute | solution.py:49
  65.6 4.4 %collective-permute-start.2 = (f32[32,256]{1,0:T(8,128)S(1)}, f32[32,256]{1,0:T(8,128)S(1)}, u32[]{:S(2)}, u32[]{:S(2)}) collective-permute-start(f32[32,256]{1,0:T(8,128)S(1)} %add.41), channel_id=1, source_target_pairs={{0,2},{2,0},{4,6},{6,4},{8,10},{10,8},{12,14},{14,12},{16,18},{18,... | collective-permute-start | bytes 98312 | tf_op jit(solution)/shard_map/ppermute | solution.py:49
  70.0 10.5 %collective-permute-start.7 = (f32[32,256]{1,0:T(8,128)S(1)}, f32[32,256]{1,0:T(8,128)S(1)}, u32[]{:S(2)}, u32[]{:S(2)}) collective-permute-start(f32[32,256]{1,0:T(8,128)S(1)} %add_add_fusion.1.refs_0_), channel_id=1, source_target_pairs={{0,24},{2,26},{4,28},{6,30},{8,16},{10,18},{12,20},{14,22},{16,8},... | collective-permute-start | bytes 98312 | tf_op jit(solution)/shard_map/ppermute | solution.py:49
  73.3 7.8 %collective-permute-start.6 = (f32[32,256]{1,0:T(8,128)S(1)}, f32[32,256]{1,0:T(8,128)S(1)}, u32[]{:S(2)}, u32[]{:S(2)}) collective-permute-start(f32[32,256]{1,0:T(8,128)S(1)} %add_add_fusion.1.refs_0_), channel_id=1, source_target_pairs={{0,16},{2,18},{4,20},{6,22},{8,24},{10,26},{12,28},{14,30},{16,0},... | collective-permute-start | bytes 98312 | tf_op jit(solution)/shard_map/ppermute | solution.py:49
  73.3 8.4 %collective-permute-start.5 = (f32[32,256]{1,0:T(8,128)S(1)}, f32[32,256]{1,0:T(8,128)S(1)}, u32[]{:S(2)}, u32[]{:S(2)}) collective-permute-start(f32[32,256]{1,0:T(8,128)S(1)} %add_add_fusion.1.refs_0_), channel_id=1, source_target_pairs={{0,8},{2,10},{4,12},{6,14},{8,0},{10,2},{12,4},{14,6},{16,24},{18,... | collective-permute-start | bytes 98312 | tf_op jit(solution)/shard_map/ppermute | solution.py:49
  80.5 0.6 copy-start.9
  81.1 0.6 copy-start.11
  81.7 0.6 copy-start.13
  82.4 0.9 copy-start.6
  83.3 0.8 copy-start.10
  84.0 0.8 copy-start.12
  84.8 0.8 copy-start.14
  85.5 0.7 copy-start.18
  86.2 0.7 copy-start.21
  86.9 0.7 copy-start.23
  87.5 13.9 %copy-start.19 = (s32[40]{0:T(128)S(1)}, s32[40]{0:T(128)}, u32[]{:S(2)}) copy-start(s32[40]{0:T(128)} %copy-done.17) | copy-start | bytes 484
  87.5 13.9 %copy-start.22 = (s32[1,1,40]{2,1,0:T(1,128)S(1)}, s32[1,1,40]{2,1,0:T(1,128)}, u32[]{:S(2)}) copy-start(s32[1,1,40]{2,1,0:T(1,128)} %param.6) | copy-start | bytes 484
  98.0 0.7 copy-start.7
  98.7 36.3 %copy-start.8 = (f32[32,1024]{1,0:T(8,128)S(1)}, f32[32,1024]{1,0:T(8,128)}, u32[]{:S(2)}) copy-start(f32[32,1024]{1,0:T(8,128)} %copy-done.7) | copy-start | bytes 393220
  98.7 36.3 %copy-start.16 = (s32[16]{0:T(128)S(1)}, s32[16]{0:T(128)}, u32[]{:S(2)}) copy-start(s32[16]{0:T(128)} %copy-done.15) | copy-start | bytes 196
  98.7 36.4 %copy-start.24 = (s32[16]{0:T(128)S(1)}, s32[16]{0:T(128)}, u32[]{:S(2)}) copy-start(s32[16]{0:T(128)} %targets.3) | copy-start | bytes 196
  98.7 2.8 %collective-permute-start.8 = (f32[128,2176]{1,0:T(8,128)S(1)}, f32[128,2176]{1,0:T(8,128)S(1)}, u32[]{:S(2)}, u32[]{:S(2)}) collective-permute-start(f32[128,2176]{1,0:T(8,128)S(1)} %get-tuple-element.28.refs_0_), channel_id=1, source_target_pairs={{0,1},{1,0},{2,3},{3,2},{4,5},{5,4},{6,7},{7,6},{8,9},{9,8},{10,11... | collective-permute-start | bytes 3342344 | tf_op jit(solution)/shard_map/ppermute | solution.py:49
  106.5 28.5 %all-to-all-start.3 = ((f32[16,32,128]{2,1,0:T(8,128)}), f32[16,32,128]{2,1,0:T(8,128)S(1)}, u32[]{:S(2)}, u32[]{:S(2)}) async-start(f32[16,32,128]{2,1,0:T(8,128)} %get-tuple-element.29), calls=%async_computation.3 | async-start | bytes 524288 | tf_op jit(solution)/shard_map/all_to_all | solution.py:60
  111.9 5.6 %collective-permute-start.11 = (f32[32,256]{1,0:T(8,128)S(1)}, f32[32,256]{1,0:T(8,128)S(1)}, u32[]{:S(2)}, u32[]{:S(2)}) collective-permute-start(f32[32,256]{1,0:T(8,128)S(1)} %get-tuple-element.31), channel_id=1, source_target_pairs={{0,6},{2,4},{4,2},{6,0},{8,14},{10,12},{12,10},{14,8},{16,22},{18,... | collective-permute-start | bytes 98312 | tf_op jit(solution)/shard_map/ppermute | solution.py:49
  114.8 4.1 %collective-permute-start.10 = (f32[32,256]{1,0:T(8,128)S(1)}, f32[32,256]{1,0:T(8,128)S(1)}, u32[]{:S(2)}, u32[]{:S(2)}) collective-permute-start(f32[32,256]{1,0:T(8,128)S(1)} %get-tuple-element.31), channel_id=1, source_target_pairs={{0,4},{2,6},{4,0},{6,2},{8,12},{10,14},{12,8},{14,10},{16,20},{18,... | collective-permute-start | bytes 98312 | tf_op jit(solution)/shard_map/ppermute | solution.py:49
  115.3 3.9 %collective-permute-start.9 = (f32[32,256]{1,0:T(8,128)S(1)}, f32[32,256]{1,0:T(8,128)S(1)}, u32[]{:S(2)}, u32[]{:S(2)}) collective-permute-start(f32[32,256]{1,0:T(8,128)S(1)} %get-tuple-element.31), channel_id=1, source_target_pairs={{0,2},{2,0},{4,6},{6,4},{8,10},{10,8},{12,14},{14,12},{16,18},{18,... | collective-permute-start | bytes 98312 | tf_op jit(solution)/shard_map/ppermute | solution.py:49
  119.2 5.8 %collective-permute-start.14 = (f32[32,256]{1,0:T(8,128)S(1)}, f32[32,256]{1,0:T(8,128)S(1)}, u32[]{:S(2)}, u32[]{:S(2)}) collective-permute-start(f32[32,256]{1,0:T(8,128)S(1)} %add_add_fusion.refs_0_), channel_id=1, source_target_pairs={{0,24},{2,26},{4,28},{6,30},{8,16},{10,18},{12,20},{14,22},{16,8},... | collective-permute-start | bytes 98312 | tf_op jit(solution)/shard_map/ppermute | solution.py:49
  122.9 4.8 %collective-permute-start.13 = (f32[32,256]{1,0:T(8,128)S(1)}, f32[32,256]{1,0:T(8,128)S(1)}, u32[]{:S(2)}, u32[]{:S(2)}) collective-permute-start(f32[32,256]{1,0:T(8,128)S(1)} %add_add_fusion.refs_0_), channel_id=1, source_target_pairs={{0,16},{2,18},{4,20},{6,22},{8,24},{10,26},{12,28},{14,30},{16,0},... | collective-permute-start | bytes 98312 | tf_op jit(solution)/shard_map/ppermute | solution.py:49
  122.9 4.8 %collective-permute-start.12 = (f32[32,256]{1,0:T(8,128)S(1)}, f32[32,256]{1,0:T(8,128)S(1)}, u32[]{:S(2)}, u32[]{:S(2)}) collective-permute-start(f32[32,256]{1,0:T(8,128)S(1)} %add_add_fusion.refs_0_), channel_id=1, source_target_pairs={{0,8},{2,10},{4,12},{6,14},{8,0},{10,2},{12,4},{14,6},{16,24},{18,... | collective-permute-start | bytes 98312 | tf_op jit(solution)/shard_map/ppermute | solution.py:49
  136.7 1.2 collective-permute-start.15
  138.6 11.7 %all-to-all-start.4 = ((f32[16,8,128]{2,1,0:T(8,128)}), f32[16,8,128]{2,1,0:T(8,128)S(1)}, u32[]{:S(2)}, u32[]{:S(2)}) async-start(f32[16,8,128]{2,1,0:T(8,128)} %broadcast_in_dim.4), calls=%async_computation.4 | async-start | bytes 131072 | tf_op jit(solution)/shard_map/all_to_all | solution.py:60

commit v2 on v1

v2 whole, which is shorter than its diff:
```python
import functools

import jax
import jax.numpy as jnp
from jax import lax
from jax.experimental import pallas as pl
from jax.experimental.pallas import tpu as pltpu
from jax.sharding import PartitionSpec as P

OUTER = 2
INNER = 4
PAD = 8

highest = lax.Precision.HIGHEST
f32 = jnp.float32


def mm(a, b):
    return lax.dot_general(a, b, (((1,), (0,)), ((), ())), precision=highest, preferred_element_type=f32)


def mt(a, b):
    return lax.dot_general(a, b, (((1,), (1,)), ((), ())), precision=highest, preferred_element_type=f32)


def halves(x):
    high = x.astype(jnp.bfloat16)
    return high, (x - high.astype(f32)).astype(jnp.bfloat16)


def mm3(a, b):
    count = a.shape[0]
    a_high, a_low = halves(a)
    b_high, b_low = halves(b)
    dot = functools.partial(jnp.dot, preferred_element_type=f32)
    both = dot(jnp.concatenate([a_high, a_low], axis=0), b_high)
    return both[:count] + both[count:] + dot(a_high, b_low)


def lanes(values):
    return jnp.concatenate(values, axis=1)


def column(row):
    count = row.shape[1]
    eye = lax.broadcasted_iota(jnp.int32, (count, count), 0) == lax.broadcasted_iota(
        jnp.int32, (count, count), 1
    )
    return jnp.sum(jnp.where(eye, row, 0.0), axis=1, keepdims=True)


smem = pl.BlockSpec(memory_space=pltpu.SMEM)
vmem = pl.BlockSpec(memory_space=pltpu.VMEM)


def call(kernel, outs, args, scratch=(), name=None):
    specs = [smem if jnp.issubdtype(a.dtype, jnp.integer) else vmem for a in args]
    return pl.pallas_call(
        kernel,
        out_shape=tuple(jax.ShapeDtypeStruct(s, f32) for s in outs),
        in_specs=specs,
        out_specs=tuple(vmem for _ in outs),
        scratch_shapes=list(scratch),
        compiler_params=pltpu.CompilerParams(vmem_limit_bytes=12 << 20),
        name=name,
    )(*args)


def add_kernel(*refs):
    refs[-1][...] = functools.reduce(jnp.add, [p[...] for p in refs[:-1]])


def add(parts):
    if len(parts) == 1:
        return parts[0]
    return call(add_kernel, [parts[0].shape], parts, name="add")[0]


def axis_parts(x, axis):
    count = lax.axis_size(axis)
    if count & (count - 1):
        return [lax.psum(x, axis)]
    parts = [x]
    bit = 1
    while bit < count:
        x = add(parts)
        masks = (bit, 2 * bit, 3 * bit) if 2 * bit < count else (bit,)
        parts = [x] + [
            lax.ppermute(x, axis, [(i, i ^ mask) for i in range(count)]) for mask in masks
        ]
        bit *= 4
    return parts


def exchange(x, axes="row"):
    return lax.all_to_all(x, axes, split_axis=0, concat_axis=0, tiled=True)


def seg_slice(index, size):
    return pl.ds(pl.multiple_of(index * size, size), size)


def factor_inverse(gram_sum):
    count = gram_sum.shape[0]
    rows = lax.broadcasted_iota(jnp.int32, (count, count), 0)
    cols = lax.broadcasted_iota(jnp.int32, (count, count), 1)
    state = lanes([gram_sum, jnp.where(rows == cols, 1.0, 0.0)])
    below = lax.broadcasted_iota(jnp.int32, state.shape, 0)
    spread_col = lambda k: jnp.broadcast_to(state[:, k : k + 1], state.shape)
    current = spread_col(0)
    for k in range(count):
        ahead = spread_col(k + 1) if k + 1 < count else None
        factor = jnp.where(below > k, current, 0.0) * (1.0 / current[k : k + 1, :])
        if ahead is not None:
            ahead = ahead - factor * current[k + 1 : k + 2, :]
        state = state - factor * state[k : k + 1, :]
        current = ahead
    left = state[:, :count]
    diag = jnp.sum(jnp.where(rows == cols, left, 0.0), axis=1, keepdims=True)
    state = state * (1.0 / jnp.sqrt(diag))
    return jnp.where(cols >= rows, state[:, :count], 0.0), state[:, count:]


def factor(lower_inv, gram_y, top, total_rows):
    gram_image = mt(mm(lower_inv, gram_y / total_rows), lower_inv)
    upper, image_inv = factor_inverse(gram_image)
    sums = jnp.sum(upper * upper, axis=0, keepdims=True)
    scale = column(top / (sums + top))
    return lower_inv, upper, mm(image_inv, lower_inv), scale


def couple(facts, moments_vv, moments_wv, total_rows):
    lower_inv, upper, to_left, scale = facts
    bb = [mt(mm(lower_inv, m / total_rows), lower_inv) for m in moments_vv]
    rb = [
        mt(mm(to_left, m / total_rows), lower_inv) - mm(upper, b)
        for m, b in zip(moments_wv, bb)
    ]
    powers = [scale]
    for _ in range(INNER - 2):
        powers.append(powers[-1] * scale)
    couplings = []
    base = 0.0
    for m in range(INNER - 1):
        base = base + powers[m] * rb[m]
        value = base
        for k in range(m):
            value = value - powers[k] * mm(couplings[m - 1 - k], bb[k])
        couplings.append(value)
    on_basis = [lower_inv, -mm(upper, lower_inv)] + [mm(c, lower_inv) for c in couplings]
    return jnp.concatenate(on_basis, axis=0)


def correct(on_basis, to_left, scale, gain, cols_v, cols_w, cols_s):
    count = to_left.shape[0]
    mixed = mm(on_basis, cols_v)
    part = lambda k: mixed[k * count : (k + 1) * count]
    basis = part(0)
    residual = part(1) + mm(to_left, cols_w)
    correction = scale * residual
    for m in range(INNER - 1):
        correction = scale * (residual + cols_s * correction - part(2 + m))
    return basis + gain * correction


def selected(table, target_count, count):
    rows = lax.broadcasted_iota(jnp.int32, (count, 1), 0)
    chosen = jnp.zeros((count, 1), f32)
    for t in range(target_count):
        chosen = jnp.where(rows == table.target(t), 1.0, chosen)
    return chosen


class Table:
    def __init__(self, ref, row_count, tile_count, target_count):
        self.ref, self.ends = ref, []
        at = 0
        for length in (row_count, tile_count, tile_count, target_count, 1):
            self.ends.append(at)
            at += length

    def seg(self, i):
        return self.ref[self.ends[0] + i]

    def owner(self, i):
        return self.ref[self.ends[1] + i]

    def row(self, i):
        return self.ref[self.ends[2] + i]

    def target(self, i):
        return self.ref[self.ends[3] + i]

    def col(self):
        return self.ref[self.ends[4]]


def apply_tiles(tiles, table, source, image, size):
    count = tiles.shape[0]
    image[...] = jnp.zeros_like(image)

    def step(n, carry):
        image[:, seg_slice(table.row(n), size)] += mm3(source(table.owner(n)), tiles[n])
        return carry

    lax.fori_loop(0, count, step, 0, unroll=8)


def apply_back(tiles, table, image, send, vectors, size):
    count = tiles.shape[0]

    def step(n, carry):
        picked = image[:vectors, seg_slice(table.row(n), size)]
        send[table.owner(n), :vectors, :] += mm3(picked, tiles[n])
        return carry

    lax.fori_loop(0, count, step, 0, unroll=8)


def pack_kernel(dims, table, tiles, vectors, send):
    table = Table(table, *dims)
    size = tiles.shape[-1]
    count = vectors.shape[0]
    group = size // count
    rows = count // group
    gram_v = mt(vectors[...], vectors[...])
    packed = lanes([gram_v[k * rows : (k + 1) * rows] for k in range(group)])
    for r in range(send.shape[0]):
        send[r, :count, :] = vectors[:, seg_slice(table.seg(r), size)]
        send[r, count : count + rows, :] = packed
    send[:, count + rows :, :] = jnp.zeros((send.shape[0], PAD, size), f32)

    def step(n, carry):
        tile = tiles[n]
        at = slice(count + rows, count + rows + 1)
        send[table.owner(n), at, :] += jnp.sum(tile * tile, axis=0, keepdims=True)
        return carry

    lax.fori_loop(0, tiles.shape[0], step, 0, unroll=8)


def turn_kernel(tiles, turned):
    def step(n, carry):
        turned[n] = tiles[n].T
        return carry

    lax.fori_loop(0, tiles.shape[0], step, 0, unroll=4)


def unpack(packed, count):
    return jnp.concatenate(
        [packed[:, k * count : (k + 1) * count] for k in range(packed.shape[1] // count)], axis=0
    )


def first_kernel(dims, table, turned, got, image, squares):
    table = Table(table, *dims)
    size = turned.shape[-1]
    count = image.shape[0]
    rows = got.shape[1] - count - PAD
    span = image.shape[1] - size
    squares[...] = jnp.zeros_like(squares)
    packed = got[0, count : count + rows, :]
    for r in range(got.shape[0]):
        squares[:, seg_slice(table.seg(r), size)] += got[r, count + rows :, :]
        if r:
            packed = packed + got[r, count : count + rows, :]
    apply_tiles(turned, table, lambda o: got[o, :count, :], image, size)
    image[:, span : span + count] = unpack(packed, count)
    where = lax.broadcasted_iota(jnp.int32, (count, size - count), 1) == table.col()
    image[:, span + count :] = jnp.where(where, jnp.max(squares[...]), 0.0)


def first_back_kernel(dims, parts_count, table, tiles, *refs):
    table = Table(table, *dims)
    parts, (send, gram_v, image) = refs[:parts_count], refs[parts_count:]
    size = tiles.shape[-1]
    count = image.shape[0]
    span = image.shape[1] - size
    image[...] = functools.reduce(jnp.add, [p[...] for p in parts])
    top = jnp.max(image[:, span + count :])
    gram_v[...] = image[:, span:]
    gram_y = mt(image[:, :span], image[:, :span])
    corner = (lax.broadcasted_iota(jnp.int32, (count, count), 0) == 0) & (
        lax.broadcasted_iota(jnp.int32, (count, count), 1) == count - 1
    )
    gram_y = jnp.where(corner, top, gram_y)
    group = size // count
    rows = count // group
    packed = lanes([gram_y[k * rows : (k + 1) * rows] for k in range(group)])
    send[:, :count, :] = jnp.zeros((send.shape[0], count, size), f32)
    for r in range(send.shape[0]):
        send[r, count:, :] = packed
    apply_back(tiles, table, image, send, count, size)


def first_factor_kernel(total_rows, gram_v, lower_inv):
    count = gram_v.shape[0]
    lower_inv[...] = factor_inverse(gram_v[:, :count] / total_rows)[1]


def powers_of(values, scales):
    powers = [values]
    for _ in range(INNER - 1):
        powers.append(powers[-1] * scales)
    return powers


def gather_cols(got, table, cols, count, size):
    cols[...] = jnp.zeros_like(cols)
    for r in range(got.shape[0]):
        cols[:, seg_slice(table.seg(r), size)] += got[r, :count, :]


def moment_kernel(dims, table, got, vectors, squares, send, moments, small, own_w, own_s):
    table = Table(table, *dims)
    count = vectors.shape[0]
    size = got.shape[-1]
    group = size // count
    gather_cols(got, table, own_w, count, size)
    extra = got[0, count:, :]
    top = extra
    for r in range(1, got.shape[0]):
        extra = extra + got[r, count:, :]
        top = jnp.maximum(top, got[r, count:, :])
    first_row = unpack(top, count)[0:1, count - 1 : count]
    own_s[...] = squares[...] / first_row
    gram_y = unpack(extra, count)
    corner = (lax.broadcasted_iota(jnp.int32, (count, count), 0) == 0) & (
        lax.broadcasted_iota(jnp.int32, (count, count), 1) == count - 1
    )
    gram_y = jnp.where(corner, gram_y[count - 1 : count, 0:1], gram_y)
    small[...] = lanes([gram_y] + [jnp.broadcast_to(first_row, (count, count))] * (group - 1))
    for r in range(send.shape[0]):
        at = seg_slice(table.seg(r), size)
        send[r, :count, :] = own_w[:, at]
        send[r, count:, :] = own_s[:, at]
    values = vectors[...]
    both = jnp.concatenate([values, own_w[...]], axis=0)
    scales = own_s[0:1, :]
    moments[...] = jnp.zeros_like(moments)
    for j in range(1, INNER):
        values = values * scales
        found = mt(both, values)
        moments[:, (j - 1) * count : j * count] = found[:count]
        moments[:, size + (j - 1) * count : size + j * count] = found[count:]


def factor_kernel(total_rows, small, first_inv, facts):
    count = small.shape[0]
    lower_inv, upper, to_left, scale = factor(
        first_inv[...], small[:, :count], small[0:1, count : count + 1], total_rows
    )
    facts[0] = lower_inv
    facts[1] = upper
    facts[2] = to_left
    facts[3] = jnp.broadcast_to(scale, (count, count))


def second_kernel(
    dims, total_rows, parts_count, table, turned, got_v, got, vectors, own_w, own_s, small, facts, *refs
):
    table = Table(table, *dims)
    parts = refs[:parts_count]
    image, own_next, powers = refs[parts_count:]
    count = vectors.shape[0]
    size = turned.shape[-1]
    span = image.shape[1] - size
    moments = functools.reduce(jnp.add, [p[...] for p in parts])
    moments_vv = [moments[:, k * count : (k + 1) * count] for k in range(INNER - 1)]
    moments_wv = [moments[:, size + k * count : size + (k + 1) * count] for k in range(INNER - 1)]
    to_left, scale = facts[2], facts[3][:, 0:1]
    on_basis = couple((facts[0], facts[1], to_left, scale), moments_vv, moments_wv, total_rows)
    gain = selected(table, dims[2], count) / small[:, count : count + 1]
    tile_v = lanes([got_v[r, :count, :] for r in range(got.shape[0])])
    tile_w = lanes([got[r, :count, :] for r in range(got.shape[0])])
    tile_s = lanes([got[r, count : count + 1, :] for r in range(got.shape[0])])
    tile_v = correct(on_basis, to_left, scale, gain, tile_v, tile_w, tile_s)
    for k in range(INNER):
        for r in range(got.shape[0]):
            powers[r, k * count : (k + 1) * count, :] = tile_v[:, r * size : (r + 1) * size]
        if k + 1 < INNER:
            tile_v = tile_v * tile_s
    own = correct(on_basis, to_left, scale, gain, vectors[...], own_w[...], own_s[0:1, :])
    own_next[...] = own
    apply_tiles(turned, table, lambda o: powers[o], image, size)
    values = own
    for k in range(INNER):
        image[:count, span + k * count : span + (k + 1) * count] = mt(own, values)
        values = values * own_s[0:1, :]


def second_back_kernel(dims, parts_count, table, tiles, *refs):
    table = Table(table, *dims)
    parts, (send, moments, own_image, image) = refs[:parts_count], refs[parts_count:]
    size = tiles.shape[-1]
    count, width = own_image.shape
    span = image.shape[1]
    image[...] = functools.reduce(jnp.add, [p[:count, :span] for p in parts])
    moments[:, :size] = functools.reduce(jnp.add, [p[:count, span:] for p in parts])
    others = functools.reduce(jnp.add, [p[:, :span] for p in parts])
    moments[:, size:] = mt(image[...], others)
    own_image[...] = image[:, pl.ds(pl.multiple_of(table.col() * width, width), width)]
    send[...] = jnp.zeros_like(send)
    apply_back(tiles, table, image, send, count, size)


def second_factor_kernel(total_rows, parts_count, small, *refs):
    parts, (facts, triangle, on_basis) = refs[:parts_count], refs[parts_count:]
    count = small.shape[0]
    moments = functools.reduce(jnp.add, [p[...] for p in parts])
    pick = lambda k: moments[:, k * count : (k + 1) * count]
    lower_inv = factor_inverse(pick(0) / total_rows)[1]
    found = factor(lower_inv, pick(INNER), small[0:1, count : count + 1], total_rows)
    triangle[...] = found[1]
    facts[0] = found[2]
    facts[1] = jnp.broadcast_to(found[3], (count, count))
    on_basis[...] = couple(
        found,
        [pick(k) for k in range(1, INNER)],
        [pick(INNER + k) for k in range(1, INNER)],
        total_rows,
    )


def trial_kernel(dims, table, got, vectors, own_s, small, facts, on_basis, trial, send, own_w):
    table = Table(table, *dims)
    count = vectors.shape[0]
    size = got.shape[-1]
    gather_cols(got, table, own_w, count, size)
    gain = selected(table, dims[2], count) / small[:, count : count + 1]
    found = correct(
        on_basis[...], facts[0], facts[1][:, 0:1], gain, vectors[...], own_w[...], own_s[0:1, :]
    )
    trial[...] = found
    gram_sum = mt(found, found)
    rows = send.shape[1]
    packed = lanes([gram_sum[k * rows : (k + 1) * rows] for k in range(count // rows)])
    for r in range(send.shape[0]):
        send[r] = packed


def last_kernel(total_rows, got, trial, image, facts, right, left):
    count = trial.shape[0]
    packed = got[0]
    for r in range(1, got.shape[0]):
        packed = packed + got[r]
    left[...] = mm(facts[0], image[...])
    lower_inv = factor_inverse(unpack(packed, count) / total_rows)[1]
    right[...] = mm(lower_inv, trial[...])


def shards(blocks, block_rows, block_cols, start_basis, targets):
    size = blocks.shape[-1]
    tiles = blocks.reshape(-1, size, size)
    rows = block_rows.reshape(-1)
    row_count = lax.axis_size("row")
    col_count = lax.axis_size("col")
    count, width = start_basis.shape
    seg_count = width // size
    span = col_count * width
    total_rows = float(width * row_count * col_count)
    pattern = block_cols[:, 0, :]
    me_row = lax.axis_index("row")
    me_col = lax.axis_index("col")
    owners = lax.dynamic_index_in_dim(pattern, me_row, 0, keepdims=False) // seg_count
    segs = jnp.max(jnp.where(pattern // seg_count == me_row, pattern % seg_count, 0), axis=1)
    table = jnp.concatenate([segs, owners, rows, targets, me_col.reshape(1)])
    dims = (row_count, tiles.shape[0], targets.shape[0])
    packed = count * count // size

    def run(kernel, outs, args, *settings, **named):
        kernel = functools.partial(kernel, *settings)
        return call(kernel, outs, args, **named)

    (send,) = run(
        pack_kernel,
        [(row_count, count + packed + PAD, size)],
        [table, tiles, start_basis],
        dims,
        name="pack",
    )
    got_v = exchange(send)
    (turned,) = run(turn_kernel, [tiles.shape], [tiles], name="turn")
    part, squares = run(
        first_kernel,
        [(count, span + size), (PAD, width)],
        [table, turned, got_v],
        dims,
        name="first",
    )
    parts = axis_parts(part, "col")
    send, gram_v = run(
        first_back_kernel,
        [(row_count, count + packed, size), (count, size)],
        [table, tiles] + parts,
        dims,
        len(parts),
        scratch=[pltpu.VMEM((count, span + size), f32)],
        name="first_back",
    )
    got = exchange(send)
    (first_inv,) = run(
        first_factor_kernel, [(count, count)], [gram_v], total_rows, name="first_factor"
    )
    send, moments, small, own_w, own_s = run(
        moment_kernel,
        [
            (row_count, count + PAD, size),
            (count, 2 * size),
            (count, size),
            (count, width),
            (PAD, width),
        ],
        [table, got, start_basis, squares],
        dims,
        name="moments",
    )
    got = exchange(send)
    parts = axis_parts(add(axis_parts(moments, "col")), "row")
    (facts,) = run(
        factor_kernel, [(4, count, count)], [small, first_inv], total_rows, name="factor"
    )
    part, own_v = run(
        second_kernel,
        [(INNER * count, span + size), (count, width)],
        [table, turned, got_v, got, start_basis, own_w, own_s, small, facts] + parts,
        dims,
        total_rows,
        len(parts),
        scratch=[pltpu.VMEM((row_count, INNER * count, size), f32)],
        name="second",
    )
    parts = axis_parts(part, "col")
    send, moments, image = run(
        second_back_kernel,
        [(row_count, count, size), (count, 2 * size), (count, width)],
        [table, tiles] + parts,
        dims,
        len(parts),
        scratch=[pltpu.VMEM((count, span), f32)],
        name="second_back",
    )
    got = exchange(send)
    parts = axis_parts(moments, "row")
    facts, triangle, on_basis = run(
        second_factor_kernel,
        [(2, count, count), (count, count), ((INNER + 1) * count, count)],
        [small] + parts,
        total_rows,
        len(parts),
        name="second_factor",
    )
    trial, send = run(
        trial_kernel,
        [(count, width), (row_count * col_count, packed, size)],
        [table, got, own_v, own_s, small, facts, on_basis],
        dims,
        scratch=[pltpu.VMEM((count, width), f32)],
        name="trial",
    )
    got = exchange(send, ("row", "col"))
    right, left = run(
        last_kernel,
        [(count, width), (count, width)],
        [got, trial, image, facts],
        total_rows,
        name="last",
    )
    return right, left, triangle


def solution(mesh):
    in_specs = (
        P("row", "col", None, None, None),
        P("row", "col", None),
        P(None, "col", None),
        P(None, ("row", "col")),
        P(),
    )
    out_specs = (P(None, ("row", "col")), P(None, ("row", "col")), P())
    return jax.shard_map(shards, mesh=mesh, in_specs=in_specs, out_specs=out_specs, check_vma=False)
```

time: 155 us -> 142 us (0.916)
  Pallas kernels: 46.6 us -> 31.9 us
  waiting for transfers between devices: 36.9 us -> 26.7 us
  blocking collectives: 17.5 us -> 26.3 us
  local copies, waits for them, and re-layouts: 13 us -> 19.8 us
  starting transfers between devices: 37.8 us -> 34 us
    pallas_call x10 -> x15, Pallas kernels: 46.6 us -> 31.9 us  [call(): pl.pallas_call(kernel, out_shape=tuple((jax.ShapeDtypeStruct(s, f32) for...]
    all_to_all x1 -> x2, blocking collectives: 17.5 us -> 26.3 us  [exchange(): return lax.all_to_all(x, axes, split_axis=0, concat_axis=0, tiled=True)]
    all_to_all x4 -> x3, waiting for transfers between devices: 18.2 us -> 9.78 us  [exchange(): return lax.all_to_all(x, axes, split_axis=0, concat_axis=0, tiled=True)]
    unnamed x50 -> x56, local copies, waits for them, and re-layouts: 11.7 us -> 19 us
    all_to_all x4 -> x3, starting transfers between devices: 21.7 us -> 17.8 us  [exchange(): return lax.all_to_all(x, axes, split_axis=0, concat_axis=0, tiled=True)]
    ppermute x16 -> x15, waiting for transfers between devices: 18.7 us -> 16.9 us  [axis_parts(): lax.ppermute(x, axis, [(i, i ^ mask) for i in range(count)])]
    ppermute x16 -> x15, starting transfers between devices: 16.1 us -> 16.1 us  [axis_parts(): lax.ppermute(x, axis, [(i, i ^ mask) for i in range(count)])]
  transfers between devices with their start and end apart: 20 -> 18, of which waited for: 14 -> 12; matrix products, arithmetic and copies ran while one was open for 0% -> 0% of each run, Pallas kernels for 9% -> 7%
where the time goes in v2:
time: 142 us; the launch traced here: 141 us
  starting transfers between devices  34 us (24%)
  Pallas kernels  31.9 us (22%)
  waiting for transfers between devices  26.7 us (19%)
  blocking collectives  26.3 us (19%)
  local copies, waits for them, and re-layouts  19.8 us (14%)
  other arithmetic  1.49 us (1%)
    pallas_call x15, Pallas kernels, call(): pl.pallas_call(kernel, out_shape=tuple((jax.ShapeDtypeStruct(s, f32) for...  31.9 us
    all_to_all x2, blocking collectives, exchange(): return lax.all_to_all(x, axes, split_axis=0, concat_axis=0, tiled=True)  26.3 us
    unnamed x56, local copies, waits for them, and re-layouts  19 us
    all_to_all x3, starting transfers between devices, exchange(): return lax.all_to_all(x, axes, split_axis=0, concat_axis=0, tiled=True)  17.8 us
    ppermute x15, waiting for transfers between devices, axis_parts(): lax.ppermute(x, axis, [(i, i ^ mask) for i in range(count)])  16.9 us
    ppermute x15, starting transfers between devices, axis_parts(): lax.ppermute(x, axis, [(i, i ^ mask) for i in range(count)])  16.1 us
    all_to_all x3, waiting for transfers between devices, exchange(): return lax.all_to_all(x, axes, split_axis=0, concat_axis=0, tiled=True)  9.78 us
  transfers between devices with their start and end apart: 18, of which 12 were waited for; matrix products, arithmetic and copies ran while one was open for 0% of the time, Pallas kernels for 7%

profile of v2, /device:TPU:0, one launch (start us, length us, event | category | flops | bytes accessed | tf_op | source)
XLA Modules:
  0.0 140.9 jit_solution(16538990069124273036)
XLA Ops:
  0.6 0.7 and_select_fusion
  1.3 0.8 fusion.2
  2.1 0.7 concatenate.3.table
  2.9 1.7 %copy-done = f32[1,1,40,128,128]{4,3,2,1,0:T(8,128)S(1)} copy-done((f32[1,1,40,128,128]{4,3,2,1,0:T(8,128)S(1)}, f32[1,1,40,128,128]{4,3,2,1,0:T(8,128)}, u32[]{:S(2)}) %copy-start) | copy-done | bytes 2621464
  4.6 0.9 copy-done.5
  5.5 1.9 %pack.1 = f32[16,48,128]{2,1,0:T(8,128)} custom-call(s32[113]{0:T(128)S(1)} %concatenate.3.table, f32[40,128,128]{2,1,0:T(8,128)S(1)} %bitcast.12, f32[32,1024]{1,0:T(8,128)S(1)} %copy-done.5), custom_call_target="tpu_custom_call" | custom-call | tf_op jit(solution)/shard_map/pack/pallas_call | solution.py:58
  7.4 8.3 %all-to-all-start = ((f32[16,48,128]{2,1,0:T(8,128)}), f32[16,48,128]{2,1,0:T(8,128)S(1)}, u32[]{:S(2)}, u32[]{:S(2)}) async-start(f32[16,48,128]{2,1,0:T(8,128)} %pack.1), calls=%async_computation | async-start | bytes 786432 | tf_op jit(solution)/shard_map/all_to_all | solution.py:96
  15.8 1.3 turn.1.turned
  17.1 1.5 %copy-done.2 = f32[40,128,128]{2,1,0:T(8,128)} copy-done((f32[40,128,128]{2,1,0:T(8,128)}, f32[40,128,128]{2,1,0:T(8,128)S(1)}, u32[]{:S(2)}) %copy-start.2) | copy-done | bytes 2621464
  18.6 9.8 %all-to-all-done.got.got_v = f32[16,48,128]{2,1,0:T(8,128)S(1)} async-done(((f32[16,48,128]{2,1,0:T(8,128)}), f32[16,48,128]{2,1,0:T(8,128)S(1)}, u32[]{:S(2)}, u32[]{:S(2)}) %all-to-all-start) | async-done | bytes 393248 | tf_op jit(solution)/shard_map/all_to_all | solution.py:96
  28.4 1.7 %copy-done.3 = f32[40,128,128]{2,1,0:T(8,128)S(1)} copy-done((f32[40,128,128]{2,1,0:T(8,128)S(1)}, f32[40,128,128]{2,1,0:T(8,128)}, u32[]{:S(2)}) %copy-start.3) | copy-done | bytes 2621464
  30.1 2.0 %first.1 = (f32[32,2176]{1,0:T(8,128)S(1)}, f32[8,1024]{1,0:T(8,128)S(1)}) custom-call(s32[113]{0:T(128)S(1)} %concatenate.3.table, f32[40,128,128]{2,1,0:T(8,128)S(1)} %copy-done.3, f32[16,48,128]{2,1,0:T(8,128)S(1)} %all-to-all-done.got.got_v), custom_call_target="tpu_custom_call" | custom-call | tf_op jit(solution)/shard_map/first/pallas_call | solution.py:58
  32.2 1.5 %collective-permute-done.refs_1_ = f32[32,2176]{1,0:T(8,128)S(1)} collective-permute-done((f32[32,2176]{1,0:T(8,128)S(1)}, f32[32,2176]{1,0:T(8,128)S(1)}, u32[]{:S(2)}, u32[]{:S(2)}) %collective-permute-start) | collective-permute-done | bytes 278560 | tf_op jit(solution)/shard_map/ppermute | solution.py:89
  33.8 2.3 %first_back.1 = (f32[16,40,128]{2,1,0:T(8,128)S(1)}, f32[32,128]{1,0:T(8,128)S(1)}) custom-call(s32[113]{0:T(128)S(1)} %concatenate.3.table, f32[40,128,128]{2,1,0:T(8,128)S(1)} %bitcast.14, f32[32,2176]{1,0:T(8,128)S(1)} %get-tuple-element.24.refs_0_, f32[32,2176]{1,0:T(8,128)S(1)} %collective-permute-done.refs_1_), custom_call_target="tpu_custom_call" | custom-call | tf_op jit(solution)/shard_map/first_back/pallas_call | solution.py:58
  36.1 0.6 copy-done.26
  36.7 15.0 %all_to_all.25.got = f32[16,40,128]{2,1,0:T(8,128)S(1)} all-to-all(f32[16,40,128]{2,1,0:T(8,128)S(1)} %get-tuple-element.25), channel_id=1, replica_groups=mesh['row'=16,'col'=2] {'row'}, dimensions={0} | all-to-all | bytes 655360 | tf_op jit(solution)/shard_map/all_to_all | solution.py:96
  51.7 1.5 %moments.1 = (f32[16,40,128]{2,1,0:T(8,128)S(1)}, f32[32,256]{1,0:T(8,128)S(1)}, f32[32,128]{1,0:T(8,128)S(1)}, f32[32,1024]{1,0:T(8,128)S(1)}, f32[8,1024]{1,0:T(8,128)S(1)}) custom-call(s32[113]{0:T(128)S(1)} %concatenate.3.table, f32[16,40,128]{2,1,0:T(8,128)S(1)} %all_to_all.25.got, f32[32,1024]{1,0:T(8,128)S(1)} %copy-done.6, ...), custom_call_target="tpu_custom_call" | custom-call | tf_op jit(solution)/shard_map/moments/pallas_call | solution.py:58
  53.2 0.7 copy-done.7
  54.0 0.6 copy-done.8
  54.6 0.7 copy-done.15
  55.2 3.5 %all-to-all-start.2 = ((f32[16,40,128]{2,1,0:T(8,128)}), f32[16,40,128]{2,1,0:T(8,128)S(1)}, u32[]{:S(2)}, u32[]{:S(2)}) async-start(f32[16,40,128]{2,1,0:T(8,128)} %copy-done.7), calls=%async_computation.2 | async-start | bytes 655360 | tf_op jit(solution)/shard_map/all_to_all | solution.py:96
  58.8 0.1 collective-permute-start.1
  58.9 1.2 collective-permute-done.1.refs_1_
  60.1 2.7 %collective-permute-start.4 = (f32[32,256]{1,0:T(8,128)S(1)}, f32[32,256]{1,0:T(8,128)S(1)}, u32[]{:S(2)}, u32[]{:S(2)}) collective-permute-start(f32[32,256]{1,0:T(8,128)S(1)} %add.22.refs_0_), channel_id=1, source_target_pairs={{0,6},{2,4},{4,2},{6,0},{8,14},{10,12},{12,10},{14,8},{16,22},{18,... | collective-permute-start | bytes 98312 | tf_op jit(solution)/shard_map/ppermute | solution.py:89
  62.8 0.6 collective-permute-start.3
  63.3 0.2 collective-permute-start.2
  63.5 1.3 collective-permute-done.4.refs_3_
  64.9 2.0 %collective-permute-done.3.refs_2_ = f32[32,256]{1,0:T(8,128)S(1)} collective-permute-done((f32[32,256]{1,0:T(8,128)S(1)}, f32[32,256]{1,0:T(8,128)S(1)}, u32[]{:S(2)}, u32[]{:S(2)}) %collective-permute-start.3) | collective-permute-done | bytes 32800 | tf_op jit(solution)/shard_map/ppermute | solution.py:89
  66.8 0.4 collective-permute-done.2.refs_1_
  67.3 3.8 %collective-permute-start.7 = (f32[32,256]{1,0:T(8,128)S(1)}, f32[32,256]{1,0:T(8,128)S(1)}, u32[]{:S(2)}, u32[]{:S(2)}) collective-permute-start(f32[32,256]{1,0:T(8,128)S(1)} %add.23.refs_0_), channel_id=1, source_target_pairs={{0,24},{2,26},{4,28},{6,30},{8,16},{10,18},{12,20},{14,22},{16,8},... | collective-permute-start | bytes 98312 | tf_op jit(solution)/shard_map/ppermute | solution.py:89
  71.0 0.7 collective-permute-start.5
  71.7 0.7 copy-done.27
  72.5 1.6 %first_factor.1.first_inv = f32[32,32]{1,0:T(8,128)S(1)} custom-call(f32[32,128]{1,0:T(8,128)S(1)} %copy-done.27), custom_call_target="tpu_custom_call" | custom-call | tf_op jit(solution)/shard_map/first_factor/pallas_call | solution.py:58
  74.0 2.0 %factor.1.facts = f32[4,32,32]{2,1,0:T(8,128)S(1)} custom-call(f32[32,128]{1,0:T(8,128)S(1)} %get-tuple-element.30.small, f32[32,32]{1,0:T(8,128)S(1)} %first_factor.1.first_inv), custom_call_target="tpu_custom_call" | custom-call | tf_op jit(solution)/shard_map/factor/pallas_call | solution.py:58
  76.0 0.6 copy-done.17
  76.6 0.6 copy-done.19
  77.2 0.6 copy-done.21
  77.8 1.7 %copy-done.4 = f32[40,128,128]{2,1,0:T(8,128)S(1)} copy-done((f32[40,128,128]{2,1,0:T(8,128)S(1)}, f32[40,128,128]{2,1,0:T(8,128)}, u32[]{:S(2)}) %copy-start.4) | copy-done | bytes 2621464
  79.6 0.8 copy-done.9
  80.3 0.8 copy-done.12
  81.1 0.9 copy-done.16
  82.0 0.8 copy-done.18
  82.8 0.8 copy-done.20
  83.5 0.8 copy-done.22
  84.3 0.6 copy-done.24
  84.9 6.2 %second.1 = (f32[128,2176]{1,0:T(8,128)S(1)}, f32[32,1024]{1,0:T(8,128)S(1)}) custom-call(s32[113]{0:T(128)S(1)} %copy-done.24, f32[40,128,128]{2,1,0:T(8,128)S(1)} %copy-done.4, f32[16,48,128]{2,1,0:T(8,128)S(1)} %all-to-all-done.got.got_v, f32[16,40,128]{2,1,0:T(8,128)S(1)} %all-to-all-done.2.got, f32[32,1024]{1,0:T(8,128)S(1)} %copy-done.6, ...), custom_call_target="tpu_custom_call" | custom-call | tf_op jit(solution)/shard_map/second/pallas_call | solution.py:58
  91.2 2.7 %collective-permute-done.8.refs_1_ = f32[128,2176]{1,0:T(8,128)S(1)} collective-permute-done((f32[128,2176]{1,0:T(8,128)S(1)}, f32[128,2176]{1,0:T(8,128)S(1)}, u32[]{:S(2)}, u32[]{:S(2)}) %collective-permute-start.8) | collective-permute-done | bytes 1114144 | tf_op jit(solution)/shard_map/ppermute | solution.py:89
  94.0 3.7 %second_back.1 = (f32[16,32,128]{2,1,0:T(8,128)}, f32[32,256]{1,0:T(8,128)S(1)}, f32[32,1024]{1,0:T(8,128)S(1)}) custom-call(s32[113]{0:T(128)S(1)} %copy-done.24, f32[40,128,128]{2,1,0:T(8,128)S(1)} %bitcast.15, f32[128,2176]{1,0:T(8,128)S(1)} %get-tuple-element.33.refs_0_, f32[128,2176]{1,0:T(8,128)S(1)} %collective-permute-done.8.refs_1_), custom_call_target="tpu_custom_call" | custom-call | tf_op jit(solution)/shard_map/second_back/pallas_call | solution.py:58
  97.6 6.0 %all-to-all-start.3 = ((f32[16,32,128]{2,1,0:T(8,128)}), f32[16,32,128]{2,1,0:T(8,128)S(1)}, u32[]{:S(2)}, u32[]{:S(2)}) async-start(f32[16,32,128]{2,1,0:T(8,128)} %get-tuple-element.34), calls=%async_computation.3 | async-start | bytes 524288 | tf_op jit(solution)/shard_map/all_to_all | solution.py:96
  103.6 2.8 %collective-permute-start.11 = (f32[32,256]{1,0:T(8,128)S(1)}, f32[32,256]{1,0:T(8,128)S(1)}, u32[]{:S(2)}, u32[]{:S(2)}) collective-permute-start(f32[32,256]{1,0:T(8,128)S(1)} %get-tuple-element.36.refs_0_), channel_id=1, source_target_pairs={{0,6},{2,4},{4,2},{6,0},{8,14},{10,12},{12,10},{14,8},{16,22},{18,... | collective-permute-start | bytes 98312 | tf_op jit(solution)/shard_map/ppermute | solution.py:89
  106.4 0.6 collective-permute-start.10
  107.0 0.2 collective-permute-start.9
  107.2 2.1 %collective-permute-done.11.refs_3_ = f32[32,256]{1,0:T(8,128)S(1)} collective-permute-done((f32[32,256]{1,0:T(8,128)S(1)}, f32[32,256]{1,0:T(8,128)S(1)}, u32[]{:S(2)}, u32[]{:S(2)}) %collective-permute-start.11) | collective-permute-done | bytes 32800 | tf_op jit(solution)/shard_map/ppermute | solution.py:89
  109.2 1.3 collective-permute-done.10.refs_2_
  110.5 0.4 collective-permute-done.9.refs_1_
  110.9 3.6 %collective-permute-start.14 = (f32[32,256]{1,0:T(8,128)S(1)}, f32[32,256]{1,0:T(8,128)S(1)}, u32[]{:S(2)}, u32[]{:S(2)}) collective-permute-start(f32[32,256]{1,0:T(8,128)S(1)} %add.24.refs_0_), channel_id=1, source_target_pairs={{0,24},{2,26},{4,28},{6,30},{8,16},{10,18},{12,20},{14,22},{16,8},... | collective-permute-start | bytes 98312 | tf_op jit(solution)/shard_map/ppermute | solution.py:89
  114.5 0.8 collective-permute-start.12
  115.4 1.3 collective-permute-done.14.refs_3_
  116.7 2.6 %collective-permute-done.13.refs_2_ = f32[32,256]{1,0:T(8,128)S(1)} collective-permute-done((f32[32,256]{1,0:T(8,128)S(1)}, f32[32,256]{1,0:T(8,128)S(1)}, u32[]{:S(2)}, u32[]{:S(2)}) %collective-permute-start.13) | collective-permute-done | bytes 32800 | tf_op jit(solution)/shard_map/ppermute | solution.py:89
  119.4 5.2 %second_factor.1 = (f32[2,32,32]{2,1,0:T(8,128)S(1)}, f32[32,32]{1,0:T(8,128)}, f32[160,32]{1,0:T(8,128)S(1)}) custom-call(f32[32,128]{1,0:T(8,128)S(1)} %get-tuple-element.30.small, f32[32,256]{1,0:T(8,128)S(1)} %add.24.refs_0_, f32[32,256]{1,0:T(8,128)S(1)} %collective-permute-done.12.refs_1_, f32[32,256]{1,0:T(8,128)S(1)} %collective-permute-done.13.refs_2_, ...), custom_call_target="tpu_custom_call" | custom-call | tf_op jit(solution)/shard_map/second_factor/pallas_call | solution.py:58
  124.6 0.9 copy-done.14
  125.5 1.7 %trial.1 = (f32[32,1024]{1,0:T(8,128)S(1)}, f32[32,8,128]{2,1,0:T(8,128)S(1)}) custom-call(s32[113]{0:T(128)S(1)} %copy-done.25, f32[16,32,128]{2,1,0:T(8,128)S(1)} %all-to-all-done.3.got, f32[32,1024]{1,0:T(8,128)S(1)} %copy-done.14, f32[8,1024]{1,0:T(8,128)S(1)} %copy-done.10, f32[32,128]{1,0:T(8,128)S(1)} %get-tuple-element.30.small, ...), custom_call_target="tpu_custom_call" | custom-call | tf_op jit(solution)/shard_map/trial/pallas_call | solution.py:58
  127.2 11.3 %all_to_all.26.got = f32[32,8,128]{2,1,0:T(8,128)S(1)} all-to-all(f32[32,8,128]{2,1,0:T(8,128)S(1)} %get-tuple-element.39), channel_id=1, replica_groups=mesh['row'=16,'col'=2] {'row','col'}, dimensions={0} | all-to-all | bytes 262144 | tf_op jit(solution)/shard_map/all_to_all | solution.py:96
  138.4 2.5 %last.1 = (f32[32,1024]{1,0:T(8,128)}, f32[32,1024]{1,0:T(8,128)}) custom-call(f32[32,8,128]{2,1,0:T(8,128)S(1)} %all_to_all.26.got, f32[32,1024]{1,0:T(8,128)S(1)} %get-tuple-element.40.trial, f32[32,1024]{1,0:T(8,128)S(1)} %get-tuple-element.41.image, f32[2,32,32]{2,1,0:T(8,128)S(1)} %get-tuple-element.37.facts), custom_call_target="tpu_custom_call" | custom-call | tf_op jit(solution)/shard_map/last/pallas_call | solution.py:58
  (48 shorter events, 0.2 us)
Async XLA Ops:
  2.9 48.8 %copy-start.23 = (s32[113]{0:T(128)}, s32[113]{0:T(128)S(1)}, u32[]{:S(2)}) copy-start(s32[113]{0:T(128)S(1)} %concatenate.3.table) | copy-start | bytes 1360
  2.9 1.7 %copy-start = (f32[1,1,40,128,128]{4,3,2,1,0:T(8,128)S(1)}, f32[1,1,40,128,128]{4,3,2,1,0:T(8,128)}, u32[]{:S(2)}) copy-start(f32[1,1,40,128,128]{4,3,2,1,0:T(8,128)} %param.5) | copy-start | bytes 7864324
  4.6 0.9 copy-start.5
  5.5 10.3 %copy-start.1 = (f32[1,1,40,128,128]{4,3,2,1,0:T(8,128)S(1)}, f32[1,1,40,128,128]{4,3,2,1,0:T(8,128)}, u32[]{:S(2)}) copy-start(f32[1,1,40,128,128]{4,3,2,1,0:T(8,128)} %param.5) | copy-start | bytes 7864324
  7.4 21.0 %all-to-all-start = ((f32[16,48,128]{2,1,0:T(8,128)}), f32[16,48,128]{2,1,0:T(8,128)S(1)}, u32[]{:S(2)}, u32[]{:S(2)}) async-start(f32[16,48,128]{2,1,0:T(8,128)} %pack.1), calls=%async_computation | async-start | bytes 786432 | tf_op jit(solution)/shard_map/all_to_all | solution.py:96
  17.1 1.5 %copy-start.2 = (f32[40,128,128]{2,1,0:T(8,128)}, f32[40,128,128]{2,1,0:T(8,128)S(1)}, u32[]{:S(2)}) copy-start(f32[40,128,128]{2,1,0:T(8,128)S(1)} %turn.1.turned) | copy-start | bytes 7864324
  28.4 1.7 %copy-start.3 = (f32[40,128,128]{2,1,0:T(8,128)S(1)}, f32[40,128,128]{2,1,0:T(8,128)}, u32[]{:S(2)}) copy-start(f32[40,128,128]{2,1,0:T(8,128)} %copy-done.2) | copy-start | bytes 7864324
  32.2 19.5 %copy-start.6 = (f32[32,1024]{1,0:T(8,128)S(1)}, f32[32,1024]{1,0:T(8,128)}, u32[]{:S(2)}) copy-start(f32[32,1024]{1,0:T(8,128)} %vectors.5) | copy-start | bytes 393220
  32.2 1.6 %collective-permute-start = (f32[32,2176]{1,0:T(8,128)S(1)}, f32[32,2176]{1,0:T(8,128)S(1)}, u32[]{:S(2)}, u32[]{:S(2)}) collective-permute-start(f32[32,2176]{1,0:T(8,128)S(1)} %get-tuple-element.24.refs_0_), channel_id=1, source_target_pairs={{0,1},{1,0},{2,3},{3,2},{4,5},{5,4},{6,7},{7,6},{8,9},{9,8},{10,11... | collective-permute-start | bytes 835592 | tf_op jit(solution)/shard_map/ppermute | solution.py:89
  36.1 0.6 copy-start.26
  53.2 0.7 copy-start.7
  54.0 0.6 copy-start.8
  54.6 0.7 copy-start.15
  55.2 22.6 %all-to-all-start.2 = ((f32[16,40,128]{2,1,0:T(8,128)}), f32[16,40,128]{2,1,0:T(8,128)S(1)}, u32[]{:S(2)}, u32[]{:S(2)}) async-start(f32[16,40,128]{2,1,0:T(8,128)} %copy-done.7), calls=%async_computation.2 | async-start | bytes 655360 | tf_op jit(solution)/shard_map/all_to_all | solution.py:96
  58.8 1.3 collective-permute-start.1
  60.1 4.8 %collective-permute-start.4 = (f32[32,256]{1,0:T(8,128)S(1)}, f32[32,256]{1,0:T(8,128)S(1)}, u32[]{:S(2)}, u32[]{:S(2)}) collective-permute-start(f32[32,256]{1,0:T(8,128)S(1)} %add.22.refs_0_), channel_id=1, source_target_pairs={{0,6},{2,4},{4,2},{6,0},{8,14},{10,12},{12,10},{14,8},{16,22},{18,... | collective-permute-start | bytes 98312 | tf_op jit(solution)/shard_map/ppermute | solution.py:89
  62.8 4.1 %collective-permute-start.3 = (f32[32,256]{1,0:T(8,128)S(1)}, f32[32,256]{1,0:T(8,128)S(1)}, u32[]{:S(2)}, u32[]{:S(2)}) collective-permute-start(f32[32,256]{1,0:T(8,128)S(1)} %add.22.refs_0_), channel_id=1, source_target_pairs={{0,4},{2,6},{4,0},{6,2},{8,12},{10,14},{12,8},{14,10},{16,20},{18,... | collective-permute-start | bytes 98312 | tf_op jit(solution)/shard_map/ppermute | solution.py:89
  63.3 3.9 %collective-permute-start.2 = (f32[32,256]{1,0:T(8,128)S(1)}, f32[32,256]{1,0:T(8,128)S(1)}, u32[]{:S(2)}, u32[]{:S(2)}) collective-permute-start(f32[32,256]{1,0:T(8,128)S(1)} %add.22.refs_0_), channel_id=1, source_target_pairs={{0,2},{2,0},{4,6},{6,4},{8,10},{10,8},{12,14},{14,12},{16,18},{18,... | collective-permute-start | bytes 98312 | tf_op jit(solution)/shard_map/ppermute | solution.py:89
  67.3 9.3 %copy-start.11 = (f32[32,256]{1,0:T(8,128)}, f32[32,256]{1,0:T(8,128)S(1)}, u32[]{:S(2)}) copy-start(f32[32,256]{1,0:T(8,128)S(1)} %add.23.refs_0_) | copy-start | bytes 98308
  67.3 8.7 %collective-permute-start.7 = (f32[32,256]{1,0:T(8,128)S(1)}, f32[32,256]{1,0:T(8,128)S(1)}, u32[]{:S(2)}, u32[]{:S(2)}) collective-permute-start(f32[32,256]{1,0:T(8,128)S(1)} %add.23.refs_0_), channel_id=1, source_target_pairs={{0,24},{2,26},{4,28},{6,30},{8,16},{10,18},{12,20},{14,22},{16,8},... | collective-permute-start | bytes 98312 | tf_op jit(solution)/shard_map/ppermute | solution.py:89
  71.0 5.6 %collective-permute-start.6 = (f32[32,256]{1,0:T(8,128)S(1)}, f32[32,256]{1,0:T(8,128)S(1)}, u32[]{:S(2)}, u32[]{:S(2)}) collective-permute-start(f32[32,256]{1,0:T(8,128)S(1)} %add.23.refs_0_), channel_id=1, source_target_pairs={{0,16},{2,18},{4,20},{6,22},{8,24},{10,26},{12,28},{14,30},{16,0},... | collective-permute-start | bytes 98312 | tf_op jit(solution)/shard_map/ppermute | solution.py:89
  71.0 6.2 %collective-permute-start.5 = (f32[32,256]{1,0:T(8,128)S(1)}, f32[32,256]{1,0:T(8,128)S(1)}, u32[]{:S(2)}, u32[]{:S(2)}) collective-permute-start(f32[32,256]{1,0:T(8,128)S(1)} %add.23.refs_0_), channel_id=1, source_target_pairs={{0,8},{2,10},{4,12},{6,14},{8,0},{10,2},{12,4},{14,6},{16,24},{18,... | collective-permute-start | bytes 98312 | tf_op jit(solution)/shard_map/ppermute | solution.py:89
  71.7 0.7 copy-start.27
  76.0 0.6 copy-start.17
  76.6 0.6 copy-start.19
  77.2 0.6 copy-start.21
  77.8 1.7 %copy-start.4 = (f32[40,128,128]{2,1,0:T(8,128)S(1)}, f32[40,128,128]{2,1,0:T(8,128)}, u32[]{:S(2)}) copy-start(f32[40,128,128]{2,1,0:T(8,128)} %copy-done.2) | copy-start | bytes 7864324
  79.6 0.8 copy-start.9
  80.3 0.8 copy-start.12
  81.1 0.9 copy-start.16
  82.0 0.8 copy-start.18
  82.8 0.8 copy-start.20
  83.5 0.8 copy-start.22
  84.3 0.6 copy-start.24
  91.1 6.5 %copy-start.13 = (f32[32,1024]{1,0:T(8,128)}, f32[32,1024]{1,0:T(8,128)S(1)}, u32[]{:S(2)}) copy-start(f32[32,1024]{1,0:T(8,128)S(1)} %get-tuple-element.35.vectors) | copy-start | bytes 393220
  91.1 33.4 %copy-start.10 = (f32[8,1024]{1,0:T(8,128)S(1)}, f32[8,1024]{1,0:T(8,128)}, u32[]{:S(2)}) copy-start(f32[8,1024]{1,0:T(8,128)} %copy-done.8) | copy-start | bytes 98308
  91.1 33.4 %copy-start.25 = (s32[113]{0:T(128)S(1)}, s32[113]{0:T(128)}, u32[]{:S(2)}) copy-start(s32[113]{0:T(128)} %copy-done.23) | copy-start | bytes 1360
  91.1 2.8 %collective-permute-start.8 = (f32[128,2176]{1,0:T(8,128)S(1)}, f32[128,2176]{1,0:T(8,128)S(1)}, u32[]{:S(2)}, u32[]{:S(2)}) collective-permute-start(f32[128,2176]{1,0:T(8,128)S(1)} %get-tuple-element.33.refs_0_), channel_id=1, source_target_pairs={{0,1},{1,0},{2,3},{3,2},{4,5},{5,4},{6,7},{7,6},{8,9},{9,8},{10,11... | collective-permute-start | bytes 3342344 | tf_op jit(solution)/shard_map/ppermute | solution.py:89
  97.6 26.9 %all-to-all-start.3 = ((f32[16,32,128]{2,1,0:T(8,128)}), f32[16,32,128]{2,1,0:T(8,128)S(1)}, u32[]{:S(2)}, u32[]{:S(2)}) async-start(f32[16,32,128]{2,1,0:T(8,128)} %get-tuple-element.34), calls=%async_computation.3 | async-start | bytes 524288 | tf_op jit(solution)/shard_map/all_to_all | solution.py:96
  103.6 5.6 %collective-permute-start.11 = (f32[32,256]{1,0:T(8,128)S(1)}, f32[32,256]{1,0:T(8,128)S(1)}, u32[]{:S(2)}, u32[]{:S(2)}) collective-permute-start(f32[32,256]{1,0:T(8,128)S(1)} %get-tuple-element.36.refs_0_), channel_id=1, source_target_pairs={{0,6},{2,4},{4,2},{6,0},{8,14},{10,12},{12,10},{14,8},{16,22},{18,... | collective-permute-start | bytes 98312 | tf_op jit(solution)/shard_map/ppermute | solution.py:89
  106.4 4.1 %collective-permute-start.10 = (f32[32,256]{1,0:T(8,128)S(1)}, f32[32,256]{1,0:T(8,128)S(1)}, u32[]{:S(2)}, u32[]{:S(2)}) collective-permute-start(f32[32,256]{1,0:T(8,128)S(1)} %get-tuple-element.36.refs_0_), channel_id=1, source_target_pairs={{0,4},{2,6},{4,0},{6,2},{8,12},{10,14},{12,8},{14,10},{16,20},{18,... | collective-permute-start | bytes 98312 | tf_op jit(solution)/shard_map/ppermute | solution.py:89
  107.0 3.9 %collective-permute-start.9 = (f32[32,256]{1,0:T(8,128)S(1)}, f32[32,256]{1,0:T(8,128)S(1)}, u32[]{:S(2)}, u32[]{:S(2)}) collective-permute-start(f32[32,256]{1,0:T(8,128)S(1)} %get-tuple-element.36.refs_0_), channel_id=1, source_target_pairs={{0,2},{2,0},{4,6},{6,4},{8,10},{10,8},{12,14},{14,12},{16,18},{18,... | collective-permute-start | bytes 98312 | tf_op jit(solution)/shard_map/ppermute | solution.py:89
  110.9 5.8 %collective-permute-start.14 = (f32[32,256]{1,0:T(8,128)S(1)}, f32[32,256]{1,0:T(8,128)S(1)}, u32[]{:S(2)}, u32[]{:S(2)}) collective-permute-start(f32[32,256]{1,0:T(8,128)S(1)} %add.24.refs_0_), channel_id=1, source_target_pairs={{0,24},{2,26},{4,28},{6,30},{8,16},{10,18},{12,20},{14,22},{16,8},... | collective-permute-start | bytes 98312 | tf_op jit(solution)/shard_map/ppermute | solution.py:89
  114.5 4.8 %collective-permute-start.13 = (f32[32,256]{1,0:T(8,128)S(1)}, f32[32,256]{1,0:T(8,128)S(1)}, u32[]{:S(2)}, u32[]{:S(2)}) collective-permute-start(f32[32,256]{1,0:T(8,128)S(1)} %add.24.refs_0_), channel_id=1, source_target_pairs={{0,16},{2,18},{4,20},{6,22},{8,24},{10,26},{12,28},{14,30},{16,0},... | collective-permute-start | bytes 98312 | tf_op jit(solution)/shard_map/ppermute | solution.py:89
  114.5 4.8 %collective-permute-start.12 = (f32[32,256]{1,0:T(8,128)S(1)}, f32[32,256]{1,0:T(8,128)S(1)}, u32[]{:S(2)}, u32[]{:S(2)}) collective-permute-start(f32[32,256]{1,0:T(8,128)S(1)} %add.24.refs_0_), channel_id=1, source_target_pairs={{0,8},{2,10},{4,12},{6,14},{8,0},{10,2},{12,4},{14,6},{16,24},{18,... | collective-permute-start | bytes 98312 | tf_op jit(solution)/shard_map/ppermute | solution.py:89
  124.6 0.9 copy-start.14

commit v3 on v2

--- a/solution.py
+++ b/solution.py
@@ -1,4 +1,5 @@
 import functools
+import math
 
 import jax
 import jax.numpy as jnp
@@ -10,6 +11,7 @@
 OUTER = 2
 INNER = 4
 PAD = 8
+HINT = 1 << 31
 
 highest = lax.Precision.HIGHEST
 f32 = jnp.float32
@@ -51,19 +53,41 @@
 
 smem = pl.BlockSpec(memory_space=pltpu.SMEM)
 vmem = pl.BlockSpec(memory_space=pltpu.VMEM)
-
-
-def call(kernel, outs, args, scratch=(), name=None):
-    specs = [smem if jnp.issubdtype(a.dtype, jnp.integer) else vmem for a in args]
+hbm = pl.BlockSpec(memory_space=pltpu.HBM)
+
+
+class Hbm:
+    def __init__(self, value):
+        self.value = value
+
+
+def call(kernel, outs, args, scratch=(), name=None, cost=None):
+    def spec(arg):
+        if isinstance(arg, Hbm):
+            return hbm
+        return smem if jnp.issubdtype(arg.dtype, jnp.integer) else vmem
+
+    def out_spec(out):
+        return hbm if isinstance(out, Hbm) else smem if isinstance(out, int) else vmem
+
+    def out_shape(out):
+        if isinstance(out, int):
+            return jax.ShapeDtypeStruct((out,), jnp.int32)
+        return jax.ShapeDtypeStruct(out.value if isinstance(out, Hbm) else out, f32)
+
+    estimate = None
+    if cost is not None:
+        estimate = pl.CostEstimate(flops=cost, bytes_accessed=0, transcendentals=0)
     return pl.pallas_call(
         kernel,
-        out_shape=tuple(jax.ShapeDtypeStruct(s, f32) for s in outs),
-        in_specs=specs,
-        out_specs=tuple(vmem for _ in outs),
+        out_shape=tuple(out_shape(o) for o in outs),
+        in_specs=[spec(a) for a in args],
+        out_specs=tuple(out_spec(o) for o in outs),
         scratch_shapes=list(scratch),
-        compiler_params=pltpu.CompilerParams(vmem_limit_bytes=12 << 20),
+        compiler_params=pltpu.CompilerParams(vmem_limit_bytes=54_000_000),
+        cost_estimate=estimate,
         name=name,
-    )(*args)
+    )(*[a.value if isinstance(a, Hbm) else a for a in args])
 
 
 def add_kernel(*refs):
@@ -175,7 +199,7 @@
     def __init__(self, ref, row_count, tile_count, target_count):
         self.ref, self.ends = ref, []
         at = 0
-        for length in (row_count, tile_count, tile_count, target_count, 1):
+        for length in (row_count, tile_count, tile_count, target_count):
             self.ends.append(at)
             at += length
 
@@ -191,60 +215,112 @@
     def target(self, i):
         return self.ref[self.ends[3] + i]
 
-    def col(self):
-        return self.ref[self.ends[4]]
+
+class Tiles:
+    def __init__(self, source, held, sems):
+        self.source, self.held, self.sems = source, held, sems
+        self.chunk = held.shape[0] // sems.shape[0]
+        self.count = sems.shape[0]
+
+    def copy(self, c):
+        part = pl.ds(c * self.chunk, self.chunk)
+        return pltpu.make_async_copy(self.source.at[part], self.held.at[part], self.sems.at[c])
+
+    def start(self):
+        for c in range(self.count):
+            self.copy(c).start()
+
+    def each(self, visit, carry=0):
+        def step(c, carry):
+            self.copy(c).wait()
+            for k in range(self.chunk):
+                n = c * self.chunk + k
+                carry = visit(n, self.held[n], carry)
+            return carry
+
+        return lax.fori_loop(0, self.count, step, carry)
+
+
+def tile_scratch(shape):
+    chunk = math.gcd(shape[0], 8)
+    return [pltpu.VMEM(shape, f32), pltpu.SemaphoreType.DMA((shape[0] // chunk,))]
 
 
 def apply_tiles(tiles, table, source, image, size):
-    count = tiles.shape[0]
     image[...] = jnp.zeros_like(image)
 
-    def step(n, carry):
-        image[:, seg_slice(table.row(n), size)] += mm3(source(table.owner(n)), tiles[n])
+    def visit(n, tile, carry):
+        image[:, seg_slice(table.row(n), size)] += mm3(source(table.owner(n)), tile)
         return carry
 
-    lax.fori_loop(0, count, step, 0, unroll=8)
-
-
-def apply_back(tiles, table, image, send, vectors, size):
-    count = tiles.shape[0]
-
-    def step(n, carry):
-        picked = image[:vectors, seg_slice(table.row(n), size)]
-        send[table.owner(n), :vectors, :] += mm3(picked, tiles[n])
+    tiles.each(visit)
+
+
+def apply_back(tiles, table, image, send, size):
+    count = image.shape[0]
+
+    def visit(n, tile, carry):
+        picked = image[:, seg_slice(table.row(n), size)]
+        send[table.owner(n), :count, :] += mm3(picked, tile)
         return carry
 
-    lax.fori_loop(0, count, step, 0, unroll=8)
-
-
-def pack_kernel(dims, table, tiles, vectors, send):
-    table = Table(table, *dims)
-    size = tiles.shape[-1]
+    tiles.each(visit)
+
+
+def pack_kernel(seg_count, pattern, rows, targets, tile_source, vectors, send, table, *scratch):
+    tiles = Tiles(tile_source, *scratch)
+    tiles.start()
+    me = lax.axis_index("row")
+    row_count, tile_count = pattern.shape
+    size = tile_source.shape[-1]
     count = vectors.shape[0]
     group = size // count
-    rows = count // group
+    high = count // group
     gram_v = mt(vectors[...], vectors[...])
-    packed = lanes([gram_v[k * rows : (k + 1) * rows] for k in range(group)])
-    for r in range(send.shape[0]):
-        send[r, :count, :] = vectors[:, seg_slice(table.seg(r), size)]
-        send[r, count : count + rows, :] = packed
-    send[:, count + rows :, :] = jnp.zeros((send.shape[0], PAD, size), f32)
-
-    def step(n, carry):
-        tile = tiles[n]
-        at = slice(count + rows, count + rows + 1)
-        send[table.owner(n), at, :] += jnp.sum(tile * tile, axis=0, keepdims=True)
+    packed = lanes([gram_v[k * high : (k + 1) * high] for k in range(group)])
+    for r in range(row_count):
+        send[r, count : count + high, :] = packed
+    send[:, count + high :, :] = jnp.zeros((row_count, PAD, size), f32)
+    at = slice(count + high, count + high + 1)
+
+    def visit(n, tile, segs):
+        owner = lax.div(pattern[me, n], seg_count)
+        table[row_count + n] = owner
+        table[row_count + tile_count + n] = rows[n]
+        send[owner, at, :] += jnp.sum(tile * tile, axis=0, keepdims=True)
+        found = []
+        for r in range(row_count):
+            value = pattern[r, n]
+            mine = lax.div(value, seg_count) == me
+            found.append(jnp.where(mine, lax.rem(value, seg_count), segs[r]))
+        return tuple(found)
+
+    segs = tiles.each(visit, (jnp.int32(0),) * row_count)
+    for r in range(row_count):
+        table[r] = segs[r]
+        send[r, :count, :] = vectors[:, seg_slice(segs[r], size)]
+    for t in range(targets.shape[0]):
+        table[row_count + 2 * tile_count + t] = targets[t]
+
+
+def turn_kernel(tile_source, turned, tiles, sems, stage, out_sems):
+    tiles = Tiles(tile_source, tiles, sems)
+    tiles.start()
+    chunk = tiles.chunk
+
+    def out(c):
+        part = pl.ds(c * chunk, chunk)
+        return pltpu.make_async_copy(stage.at[part], turned.at[part], out_sems.at[c])
+
+    def visit(n, tile, carry):
+        stage[n] = tile.T
         return carry
 
-    lax.fori_loop(0, tiles.shape[0], step, 0, unroll=8)
-
-
-def turn_kernel(tiles, turned):
-    def step(n, carry):
-        turned[n] = tiles[n].T
-        return carry
-
-    lax.fori_loop(0, tiles.shape[0], step, 0, unroll=4)
+    tiles.each(visit)
+    for c in range(tiles.count):
+        out(c).start()
+    for c in range(tiles.count):
+        out(c).wait()
 
 
 def unpack(packed, count):
@@ -253,8 +329,10 @@
     )
 
 
-def first_kernel(dims, table, turned, got, image, squares):
+def first_kernel(dims, table, turned, got, image, squares, *scratch):
     table = Table(table, *dims)
+    tiles = Tiles(turned, *scratch)
+    tiles.start()
     size = turned.shape[-1]
     count = image.shape[0]
     rows = got.shape[1] - count - PAD
@@ -265,22 +343,24 @@
         squares[:, seg_slice(table.seg(r), size)] += got[r, count + rows :, :]
         if r:
             packed = packed + got[r, count : count + rows, :]
-    apply_tiles(turned, table, lambda o: got[o, :count, :], image, size)
+    apply_tiles(tiles, table, lambda o: got[o, :count, :], image, size)
     image[:, span : span + count] = unpack(packed, count)
-    where = lax.broadcasted_iota(jnp.int32, (count, size - count), 1) == table.col()
+    where = lax.broadcasted_iota(jnp.int32, (count, size - count), 1) == lax.axis_index("col")
     image[:, span + count :] = jnp.where(where, jnp.max(squares[...]), 0.0)
 
 
-def first_back_kernel(dims, parts_count, table, tiles, *refs):
+def first_back_kernel(dims, parts_count, table, tile_source, *refs):
     table = Table(table, *dims)
-    parts, (send, gram_v, image) = refs[:parts_count], refs[parts_count:]
-    size = tiles.shape[-1]
-    count = image.shape[0]
-    span = image.shape[1] - size
-    image[...] = functools.reduce(jnp.add, [p[...] for p in parts])
-    top = jnp.max(image[:, span + count :])
-    gram_v[...] = image[:, span:]
-    gram_y = mt(image[:, :span], image[:, :span])
+    parts, (send, gram_v, image, *scratch) = refs[:parts_count], refs[parts_count:]
+    tiles = Tiles(tile_source, *scratch)
+    tiles.start()
+    size = tile_source.shape[-1]
+    count, span = image.shape
+    image[...] = functools.reduce(jnp.add, [p[:, :span] for p in parts])
+    extra = functools.reduce(jnp.add, [p[:, span:] for p in parts])
+    top = jnp.max(extra[:, count:])
+    gram_v[...] = extra
+    gram_y = mt(image[...], image[...])
     corner = (lax.broadcasted_iota(jnp.int32, (count, count), 0) == 0) & (
         lax.broadcasted_iota(jnp.int32, (count, count), 1) == count - 1
     )
@@ -291,7 +371,7 @@
     send[:, :count, :] = jnp.zeros((send.shape[0], count, size), f32)
     for r in range(send.shape[0]):
         send[r, count:, :] = packed
-    apply_back(tiles, table, image, send, count, size)
+    apply_back(tiles, table, image, send, size)
 
 
 def first_factor_kernel(total_rows, gram_v, lower_inv):
@@ -362,7 +442,9 @@
 ):
     table = Table(table, *dims)
     parts = refs[:parts_count]
-    image, own_next, powers = refs[parts_count:]
+    image, own_next, powers, *scratch = refs[parts_count:]
+    tiles = Tiles(turned, *scratch)
+    tiles.start()
     count = vectors.shape[0]
     size = turned.shape[-1]
     span = image.shape[1] - size
@@ -383,26 +465,28 @@
             tile_v = tile_v * tile_s
     own = correct(on_basis, to_left, scale, gain, vectors[...], own_w[...], own_s[0:1, :])
     own_next[...] = own
-    apply_tiles(turned, table, lambda o: powers[o], image, size)
+    apply_tiles(tiles, table, lambda o: powers[o], image, size)
     values = own
     for k in range(INNER):
         image[:count, span + k * count : span + (k + 1) * count] = mt(own, values)
         values = values * own_s[0:1, :]
 
 
-def second_back_kernel(dims, parts_count, table, tiles, *refs):
+def second_back_kernel(dims, parts_count, table, tile_source, *refs):
     table = Table(table, *dims)
-    parts, (send, moments, own_image, image) = refs[:parts_count], refs[parts_count:]
-    size = tiles.shape[-1]
+    parts, (send, moments, own_image, image, *scratch) = refs[:parts_count], refs[parts_count:]
+    tiles = Tiles(tile_source, *scratch)
+    tiles.start()
+    size = tile_source.shape[-1]
     count, width = own_image.shape
     span = image.shape[1]
     image[...] = functools.reduce(jnp.add, [p[:count, :span] for p in parts])
     moments[:, :size] = functools.reduce(jnp.add, [p[:count, span:] for p in parts])
     others = functools.reduce(jnp.add, [p[:, :span] for p in parts])
     moments[:, size:] = mt(image[...], others)
-    own_image[...] = image[:, pl.ds(pl.multiple_of(table.col() * width, width), width)]
+    own_image[...] = image[:, seg_slice(lax.axis_index("col"), width)]
     send[...] = jnp.zeros_like(send)
-    apply_back(tiles, table, image, send, count, size)
+    apply_back(tiles, table, image, send, size)
 
 
 def second_factor_kernel(total_rows, parts_count, small, *refs):
@@ -461,11 +545,6 @@
     span = col_count * width
     total_rows = float(width * row_count * col_count)
     pattern = block_cols[:, 0, :]
-    me_row = lax.axis_index("row")
-    me_col = lax.axis_index("col")
-    owners = lax.dynamic_index_in_dim(pattern, me_row, 0, keepdims=False) // seg_count
-    segs = jnp.max(jnp.where(pattern // seg_count == me_row, pattern % seg_count, 0), axis=1)
-    table = jnp.concatenate([segs, owners, rows, targets, me_col.reshape(1)])
     dims = (row_count, tiles.shape[0], targets.shape[0])
     packed = count * count // size
 
@@ -473,35 +552,40 @@
         kernel = functools.partial(kernel, *settings)
         return call(kernel, outs, args, **named)
 
-    (send,) = run(
+    held = tile_scratch(tiles.shape)
+    (send, table) = run(
         pack_kernel,
-        [(row_count, count + packed + PAD, size)],
-        [table, tiles, start_basis],
-        dims,
+        [(row_count, count + packed + PAD, size), row_count + 2 * dims[1] + dims[2]],
+        [pattern, rows, targets, Hbm(tiles), start_basis],
+        seg_count,
+        scratch=held,
         name="pack",
     )
     got_v = exchange(send)
-    (turned,) = run(turn_kernel, [tiles.shape], [tiles], name="turn")
+    (turned,) = run(
+        turn_kernel, [Hbm(tiles.shape)], [Hbm(tiles)], scratch=held + held, name="turn", cost=HINT
+    )
     part, squares = run(
         first_kernel,
         [(count, span + size), (PAD, width)],
-        [table, turned, got_v],
+        [table, Hbm(turned), got_v],
         dims,
+        scratch=held,
         name="first",
     )
     parts = axis_parts(part, "col")
     send, gram_v = run(
         first_back_kernel,
         [(row_count, count + packed, size), (count, size)],
-        [table, tiles] + parts,
+        [table, Hbm(tiles)] + parts,
         dims,
         len(parts),
-        scratch=[pltpu.VMEM((count, span + size), f32)],
+        scratch=[pltpu.VMEM((count, span), f32)] + held,
         name="first_back",
     )
     got = exchange(send)
     (first_inv,) = run(
-        first_factor_kernel, [(count, count)], [gram_v], total_rows, name="first_factor"
+        first_factor_kernel, [(count, count)], [gram_v], total_rows, name="first_factor", cost=HINT
     )
     send, moments, small, own_w, own_s = run(
         moment_kernel,
@@ -519,26 +603,26 @@
     got = exchange(send)
     parts = axis_parts(add(axis_parts(moments, "col")), "row")
     (facts,) = run(
-        factor_kernel, [(4, count, count)], [small, first_inv], total_rows, name="factor"
+        factor_kernel, [(4, count, count)], [small, first_inv], total_rows, name="factor", cost=HINT
     )
     part, own_v = run(
         second_kernel,
         [(INNER * count, span + size), (count, width)],
-        [table, turned, got_v, got, start_basis, own_w, own_s, small, facts] + parts,
+        [table, Hbm(turned), got_v, got, start_basis, own_w, own_s, small, facts] + parts,
         dims,
         total_rows,
         len(parts),
-        scratch=[pltpu.VMEM((row_count, INNER * count, size), f32)],
+        scratch=[pltpu.VMEM((row_count, INNER * count, size), f32)] + held,
         name="second",
     )
     parts = axis_parts(part, "col")
     send, moments, image = run(
         second_back_kernel,
         [(row_count, count, size), (count, 2 * size), (count, width)],
-        [table, tiles] + parts,
+        [table, Hbm(tiles)] + parts,
         dims,
         len(parts),
-        scratch=[pltpu.VMEM((count, span), f32)],
+        scratch=[pltpu.VMEM((count, span), f32)] + held,
         name="second_back",
     )
     got = exchange(send)

time: 142 us -> 132 us (0.930)
  local copies, waits for them, and re-layouts: 19.8 us -> 3.91 us
  Pallas kernels: 31.9 us -> 41.7 us
  starting transfers between devices: 34 us -> 32.4 us
  other arithmetic: 1.49 us -> 0 us
    unnamed x56 -> x12, local copies, waits for them, and re-layouts: 19 us -> 3.91 us
    pallas_call x15, Pallas kernels: 31.9 us -> 41.7 us  [call(): pl.pallas_call(kernel, out_shape=tuple((out_shape(o) for o in outs)), in_...]
    all_to_all x3, starting transfers between devices: 17.8 us -> 16.2 us  [exchange(): return lax.all_to_all(x, axes, split_axis=0, concat_axis=0, tiled=True)]
  transfers between devices with their start and end apart: 18 -> 18, of which waited for: 12 -> 12; matrix products, arithmetic and copies ran while one was open for 0% -> 0% of each run, Pallas kernels for 7% -> 9%
where the time goes in v3:
time: 132 us
  Pallas kernels  41.7 us (32%)
  starting transfers between devices  32.4 us (25%)
  waiting for transfers between devices  26.5 us (20%)
  blocking collectives  26.3 us (20%)
  local copies, waits for them, and re-layouts  3.91 us (3%)
    pallas_call x15, Pallas kernels, call(): pl.pallas_call(kernel, out_shape=tuple((out_shape(o) for o in outs)), in_...  41.7 us
    all_to_all x2, blocking collectives, exchange(): return lax.all_to_all(x, axes, split_axis=0, concat_axis=0, tiled=True)  26.3 us
    ppermute x15, waiting for transfers between devices, axis_parts(): lax.ppermute(x, axis, [(i, i ^ mask) for i in range(count)])  17.5 us
    all_to_all x3, starting transfers between devices, exchange(): return lax.all_to_all(x, axes, split_axis=0, concat_axis=0, tiled=True)  16.2 us
    ppermute x15, starting transfers between devices, axis_parts(): lax.ppermute(x, axis, [(i, i ^ mask) for i in range(count)])  16.2 us
    all_to_all x3, waiting for transfers between devices, exchange(): return lax.all_to_all(x, axes, split_axis=0, concat_axis=0, tiled=True)  8.98 us
    unnamed x12, local copies, waits for them, and re-layouts  3.91 us
  transfers between devices with their start and end apart: 18, of which 12 were waited for; matrix products, arithmetic and copies ran while one was open for 0% of the time, Pallas kernels for 9%

profile of v3, /device:TPU:0, one launch (start us, length us, event | category | flops | bytes accessed | tf_op | source)
XLA Modules:
  0.0 131.5 jit_solution(2179791579125772124)
XLA Ops:
  0.6 0.0 copy-start
  0.6 0.9 copy-done
  1.5 0.0 copy-start.2
  1.5 0.7 copy-done.2
  2.2 0.0 copy-start.3
  2.2 0.7 copy-done.3
  2.9 0.0 copy-start.4
  2.9 0.7 copy-done.4
  3.5 5.3 %pack.1 = (f32[16,48,128]{2,1,0:T(8,128)}, s32[112]{0:T(128)S(1)}) custom-call(s32[16,40]{1,0:T(8,128)S(1)} %bitcast.3, s32[40]{0:T(128)S(1)} %bitcast.4, s32[16]{0:T(128)S(1)} %copy-done.4, f32[40,128,128]{2,1,0:T(8,128)} %bitcast.5, f32[32,1024]{1,0:T(8,128)S(1)} %copy-done), custom_call_target="tpu_custom_call" | custom-call | tf_op jit(solution)/shard_map/pack/pallas_call | solution.py:81
  8.9 8.4 %all-to-all-start = ((f32[16,48,128]{2,1,0:T(8,128)}), f32[16,48,128]{2,1,0:T(8,128)S(1)}, u32[]{:S(2)}, u32[]{:S(2)}) async-start(f32[16,48,128]{2,1,0:T(8,128)} %get-tuple-element.27), calls=%async_computation | async-start | bytes 786432 | tf_op jit(solution)/shard_map/all_to_all | solution.py:120
  17.3 3.6 %turn.1.turned = f32[40,128,128]{2,1,0:T(8,128)} custom-call(f32[40,128,128]{2,1,0:T(8,128)} %bitcast.6), custom_call_target="tpu_custom_call" | custom-call | flops 2147483648 | tf_op jit(solution)/shard_map/turn/pallas_call | solution.py:81
  20.9 9.0 %all-to-all-done.got.got_v = f32[16,48,128]{2,1,0:T(8,128)S(1)} async-done(((f32[16,48,128]{2,1,0:T(8,128)}), f32[16,48,128]{2,1,0:T(8,128)S(1)}, u32[]{:S(2)}, u32[]{:S(2)}) %all-to-all-start) | async-done | bytes 393248 | tf_op jit(solution)/shard_map/all_to_all | solution.py:120
  29.9 3.1 %first.1 = (f32[32,2176]{1,0:T(8,128)S(1)}, f32[8,1024]{1,0:T(8,128)S(1)}) custom-call(s32[112]{0:T(128)S(1)} %get-tuple-element.26.table, f32[40,128,128]{2,1,0:T(8,128)} %turn.1.turned, f32[16,48,128]{2,1,0:T(8,128)S(1)} %all-to-all-done.got.got_v), custom_call_target="tpu_custom_call" | custom-call | tf_op jit(solution)/shard_map/first/pallas_call | solution.py:81
  33.0 0.0 copy-start.1
  33.0 0.1 collective-permute-start
  33.1 1.5 %collective-permute-done.refs_1_ = f32[32,2176]{1,0:T(8,128)S(1)} collective-permute-done((f32[32,2176]{1,0:T(8,128)S(1)}, f32[32,2176]{1,0:T(8,128)S(1)}, u32[]{:S(2)}, u32[]{:S(2)}) %collective-permute-start) | collective-permute-done | bytes 278560 | tf_op jit(solution)/shard_map/ppermute | solution.py:113
  34.6 3.0 %first_back.1 = (f32[16,40,128]{2,1,0:T(8,128)S(1)}, f32[32,128]{1,0:T(8,128)S(1)}) custom-call(s32[112]{0:T(128)S(1)} %get-tuple-element.26.table, f32[40,128,128]{2,1,0:T(8,128)} %bitcast.7, f32[32,2176]{1,0:T(8,128)S(1)} %get-tuple-element.28.refs_0_, f32[32,2176]{1,0:T(8,128)S(1)} %collective-permute-done.refs_1_), custom_call_target="tpu_custom_call" | custom-call | tf_op jit(solution)/shard_map/first_back/pallas_call | solution.py:81
  37.6 15.0 %all_to_all.25.got = f32[16,40,128]{2,1,0:T(8,128)S(1)} all-to-all(f32[16,40,128]{2,1,0:T(8,128)S(1)} %get-tuple-element.29), channel_id=1, replica_groups=mesh['row'=16,'col'=2] {'row'}, dimensions={0} | all-to-all | bytes 655360 | tf_op jit(solution)/shard_map/all_to_all | solution.py:120
  52.6 0.0 copy-done.1
  52.6 2.2 %moments.1 = (f32[16,40,128]{2,1,0:T(8,128)}, f32[32,256]{1,0:T(8,128)S(1)}, f32[32,128]{1,0:T(8,128)S(1)}, f32[32,1024]{1,0:T(8,128)S(1)}, f32[8,1024]{1,0:T(8,128)S(1)}) custom-call(s32[112]{0:T(128)S(1)} %get-tuple-element.26.table, f32[16,40,128]{2,1,0:T(8,128)S(1)} %all_to_all.25.got, f32[32,1024]{1,0:T(8,128)S(1)} %copy-done.1, ...), custom_call_target="tpu_custom_call" | custom-call | tf_op jit(solution)/shard_map/moments/pallas_call | solution.py:81
  54.8 3.5 %all-to-all-start.2 = ((f32[16,40,128]{2,1,0:T(8,128)}), f32[16,40,128]{2,1,0:T(8,128)S(1)}, u32[]{:S(2)}, u32[]{:S(2)}) async-start(f32[16,40,128]{2,1,0:T(8,128)} %get-tuple-element.31), calls=%async_computation.2 | async-start | bytes 655360 | tf_op jit(solution)/shard_map/all_to_all | solution.py:120
  58.3 0.1 collective-permute-start.1
  58.4 1.2 collective-permute-done.1.refs_1_
  59.6 2.7 %collective-permute-start.4 = (f32[32,256]{1,0:T(8,128)S(1)}, f32[32,256]{1,0:T(8,128)S(1)}, u32[]{:S(2)}, u32[]{:S(2)}) collective-permute-start(f32[32,256]{1,0:T(8,128)S(1)} %add.3.refs_0_), channel_id=1, source_target_pairs={{0,6},{2,4},{4,2},{6,0},{8,14},{10,12},{12,10},{14,8},{16,22},{18,... | collective-permute-start | bytes 98312 | tf_op jit(solution)/shard_map/ppermute | solution.py:113
  62.3 0.6 collective-permute-start.3
  62.9 0.2 collective-permute-start.2
  63.1 1.6 %first_factor.1.first_inv = f32[32,32]{1,0:T(8,128)S(1)} custom-call(f32[32,128]{1,0:T(8,128)S(1)} %get-tuple-element.35.gram_v), custom_call_target="tpu_custom_call" | custom-call | flops 2147483648 | tf_op jit(solution)/shard_map/first_factor/pallas_call | solution.py:81
  64.7 0.0 collective-permute-done.4.refs_3_
  64.7 1.7 %collective-permute-done.3.refs_2_ = f32[32,256]{1,0:T(8,128)S(1)} collective-permute-done((f32[32,256]{1,0:T(8,128)S(1)}, f32[32,256]{1,0:T(8,128)S(1)}, u32[]{:S(2)}, u32[]{:S(2)}) %collective-permute-start.3) | collective-permute-done | bytes 32800 | tf_op jit(solution)/shard_map/ppermute | solution.py:113
  66.4 0.4 collective-permute-done.2.refs_1_
  66.8 3.8 %collective-permute-start.7 = (f32[32,256]{1,0:T(8,128)S(1)}, f32[32,256]{1,0:T(8,128)S(1)}, u32[]{:S(2)}, u32[]{:S(2)}) collective-permute-start(f32[32,256]{1,0:T(8,128)S(1)} %add.4.refs_0_), channel_id=1, source_target_pairs={{0,24},{2,26},{4,28},{6,30},{8,16},{10,18},{12,20},{14,22},{16,8},... | collective-permute-start | bytes 98312 | tf_op jit(solution)/shard_map/ppermute | solution.py:113
  70.6 0.0 collective-permute-start.6
  70.6 0.7 collective-permute-start.5
  71.3 2.0 %factor.1.facts = f32[4,32,32]{2,1,0:T(8,128)S(1)} custom-call(f32[32,128]{1,0:T(8,128)S(1)} %get-tuple-element.34.small, f32[32,32]{1,0:T(8,128)S(1)} %first_factor.1.first_inv), custom_call_target="tpu_custom_call" | custom-call | flops 2147483648 | tf_op jit(solution)/shard_map/factor/pallas_call | solution.py:81
  73.2 0.0 collective-permute-done.7.refs_3_
  73.2 2.2 %collective-permute-done.6.refs_2_ = f32[32,256]{1,0:T(8,128)S(1)} collective-permute-done((f32[32,256]{1,0:T(8,128)S(1)}, f32[32,256]{1,0:T(8,128)S(1)}, u32[]{:S(2)}, u32[]{:S(2)}) %collective-permute-start.6) | collective-permute-done | bytes 32800 | tf_op jit(solution)/shard_map/ppermute | solution.py:113
  75.4 0.0 collective-permute-done.5.refs_1_
  75.4 0.0 all-to-all-done.2.got
  75.4 6.4 %second.1 = (f32[128,2176]{1,0:T(8,128)S(1)}, f32[32,1024]{1,0:T(8,128)S(1)}) custom-call(s32[112]{0:T(128)S(1)} %get-tuple-element.26.table, f32[40,128,128]{2,1,0:T(8,128)} %turn.1.turned, f32[16,48,128]{2,1,0:T(8,128)S(1)} %all-to-all-done.got.got_v, f32[16,40,128]{2,1,0:T(8,128)S(1)} %all-to-all-done.2.got, f32[32,1024]{1,0:T(8,128)S(1)} %copy-done.1, ...), custom_call_target="tpu_custom_call" | custom-call | tf_op jit(solution)/shard_map/second/pallas_call | solution.py:81
  81.8 0.1 collective-permute-start.8
  81.9 2.7 %collective-permute-done.8.refs_1_ = f32[128,2176]{1,0:T(8,128)S(1)} collective-permute-done((f32[128,2176]{1,0:T(8,128)S(1)}, f32[128,2176]{1,0:T(8,128)S(1)}, u32[]{:S(2)}, u32[]{:S(2)}) %collective-permute-start.8) | collective-permute-done | bytes 1114144 | tf_op jit(solution)/shard_map/ppermute | solution.py:113
  84.7 0.0 copy-start.5
  84.7 1.0 copy-done.5
  85.7 5.2 %second_back.1 = (f32[16,32,128]{2,1,0:T(8,128)}, f32[32,256]{1,0:T(8,128)S(1)}, f32[32,1024]{1,0:T(8,128)S(1)}) custom-call(s32[112]{0:T(128)S(1)} %get-tuple-element.26.table, f32[40,128,128]{2,1,0:T(8,128)} %bitcast.8, f32[128,2176]{1,0:T(8,128)S(1)} %get-tuple-element.37.refs_0_, f32[128,2176]{1,0:T(8,128)} %copy-done.5), custom_call_target="tpu_custom_call" | custom-call | tf_op jit(solution)/shard_map/second_back/pallas_call | solution.py:81
  90.8 4.3 %all-to-all-start.3 = ((f32[16,32,128]{2,1,0:T(8,128)}), f32[16,32,128]{2,1,0:T(8,128)S(1)}, u32[]{:S(2)}, u32[]{:S(2)}) async-start(f32[16,32,128]{2,1,0:T(8,128)} %get-tuple-element.38), calls=%async_computation.3 | async-start | bytes 524288 | tf_op jit(solution)/shard_map/all_to_all | solution.py:120
  95.1 2.8 %collective-permute-start.11 = (f32[32,256]{1,0:T(8,128)S(1)}, f32[32,256]{1,0:T(8,128)S(1)}, u32[]{:S(2)}, u32[]{:S(2)}) collective-permute-start(f32[32,256]{1,0:T(8,128)S(1)} %get-tuple-element.40.refs_0_), channel_id=1, source_target_pairs={{0,6},{2,4},{4,2},{6,0},{8,14},{10,12},{12,10},{14,8},{16,22},{18,... | collective-permute-start | bytes 98312 | tf_op jit(solution)/shard_map/ppermute | solution.py:113
  98.0 0.6 collective-permute-start.10
  98.5 0.2 collective-permute-start.9
  98.7 2.1 %collective-permute-done.11.refs_3_ = f32[32,256]{1,0:T(8,128)S(1)} collective-permute-done((f32[32,256]{1,0:T(8,128)S(1)}, f32[32,256]{1,0:T(8,128)S(1)}, u32[]{:S(2)}, u32[]{:S(2)}) %collective-permute-start.11) | collective-permute-done | bytes 32800 | tf_op jit(solution)/shard_map/ppermute | solution.py:113
  100.8 1.3 collective-permute-done.10.refs_2_
  102.1 0.4 collective-permute-done.9.refs_1_
  102.5 3.6 %collective-permute-start.14 = (f32[32,256]{1,0:T(8,128)S(1)}, f32[32,256]{1,0:T(8,128)S(1)}, u32[]{:S(2)}, u32[]{:S(2)}) collective-permute-start(f32[32,256]{1,0:T(8,128)S(1)} %add.5.refs_0_), channel_id=1, source_target_pairs={{0,24},{2,26},{4,28},{6,30},{8,16},{10,18},{12,20},{14,22},{16,8},... | collective-permute-start | bytes 98312 | tf_op jit(solution)/shard_map/ppermute | solution.py:113
  106.1 0.0 collective-permute-start.13
  106.1 0.8 collective-permute-start.12
  106.9 1.3 %collective-permute-done.14.refs_3_ = f32[32,256]{1,0:T(8,128)S(1)} collective-permute-done((f32[32,256]{1,0:T(8,128)S(1)}, f32[32,256]{1,0:T(8,128)S(1)}, u32[]{:S(2)}, u32[]{:S(2)}) %collective-permute-start.14) | collective-permute-done | bytes 32800 | tf_op jit(solution)/shard_map/ppermute | solution.py:113
  108.2 2.6 %collective-permute-done.13.refs_2_ = f32[32,256]{1,0:T(8,128)S(1)} collective-permute-done((f32[32,256]{1,0:T(8,128)S(1)}, f32[32,256]{1,0:T(8,128)S(1)}, u32[]{:S(2)}, u32[]{:S(2)}) %collective-permute-start.13) | collective-permute-done | bytes 32800 | tf_op jit(solution)/shard_map/ppermute | solution.py:113
  110.9 0.0 collective-permute-done.12.refs_1_
  110.9 5.2 %second_factor.1 = (f32[2,32,32]{2,1,0:T(8,128)S(1)}, f32[32,32]{1,0:T(8,128)}, f32[160,32]{1,0:T(8,128)S(1)}) custom-call(f32[32,128]{1,0:T(8,128)S(1)} %get-tuple-element.34.small, f32[32,256]{1,0:T(8,128)S(1)} %add.5.refs_0_, f32[32,256]{1,0:T(8,128)S(1)} %collective-permute-done.12.refs_1_, f32[32,256]{1,0:T(8,128)S(1)} %collective-permute-done.13.refs_2_, ...), custom_call_target="tpu_custom_call" | custom-call | tf_op jit(solution)/shard_map/second_factor/pallas_call | solution.py:81
  116.1 0.0 all-to-all-done.3.got
  116.1 1.7 %trial.1 = (f32[32,1024]{1,0:T(8,128)S(1)}, f32[32,8,128]{2,1,0:T(8,128)S(1)}) custom-call(s32[112]{0:T(128)S(1)} %get-tuple-element.26.table, f32[16,32,128]{2,1,0:T(8,128)S(1)} %all-to-all-done.3.got, f32[32,1024]{1,0:T(8,128)S(1)} %get-tuple-element.39.vectors, f32[8,1024]{1,0:T(8,128)S(1)} %get-tuple-element.33.own_s, ...), custom_call_target="tpu_custom_call" | custom-call | tf_op jit(solution)/shard_map/trial/pallas_call | solution.py:81
  117.8 11.2 %all_to_all.26.got = f32[32,8,128]{2,1,0:T(8,128)S(1)} all-to-all(f32[32,8,128]{2,1,0:T(8,128)S(1)} %get-tuple-element.43), channel_id=1, replica_groups=mesh['row'=16,'col'=2] {'row','col'}, dimensions={0} | all-to-all | bytes 262144 | tf_op jit(solution)/shard_map/all_to_all | solution.py:120
  129.1 2.5 %last.1 = (f32[32,1024]{1,0:T(8,128)}, f32[32,1024]{1,0:T(8,128)}) custom-call(f32[32,8,128]{2,1,0:T(8,128)S(1)} %all_to_all.26.got, f32[32,1024]{1,0:T(8,128)S(1)} %get-tuple-element.44.trial, f32[32,1024]{1,0:T(8,128)S(1)} %get-tuple-element.45.image, f32[2,32,32]{2,1,0:T(8,128)S(1)} %get-tuple-element.41.facts), custom_call_target="tpu_custom_call" | custom-call | tf_op jit(solution)/shard_map/last/pallas_call | solution.py:81
  (3 shorter events, 0.0 us)
Async XLA Ops:
  0.6 0.9 copy-start
  1.5 0.7 copy-start.2
  2.2 0.7 copy-start.3
  2.9 0.7 copy-start.4
  8.9 21.0 %all-to-all-start = ((f32[16,48,128]{2,1,0:T(8,128)}), f32[16,48,128]{2,1,0:T(8,128)S(1)}, u32[]{:S(2)}, u32[]{:S(2)}) async-start(f32[16,48,128]{2,1,0:T(8,128)} %get-tuple-element.27), calls=%async_computation | async-start | bytes 786432 | tf_op jit(solution)/shard_map/all_to_all | solution.py:120
  33.0 19.6 %copy-start.1 = (f32[32,1024]{1,0:T(8,128)S(1)}, f32[32,1024]{1,0:T(8,128)}, u32[]{:S(2)}) copy-start(f32[32,1024]{1,0:T(8,128)} %vectors.5) | copy-start | bytes 393220
  33.0 1.6 %collective-permute-start = (f32[32,2176]{1,0:T(8,128)S(1)}, f32[32,2176]{1,0:T(8,128)S(1)}, u32[]{:S(2)}, u32[]{:S(2)}) collective-permute-start(f32[32,2176]{1,0:T(8,128)S(1)} %get-tuple-element.28.refs_0_), channel_id=1, source_target_pairs={{0,1},{1,0},{2,3},{3,2},{4,5},{5,4},{6,7},{7,6},{8,9},{9,8},{10,11... | collective-permute-start | bytes 835592 | tf_op jit(solution)/shard_map/ppermute | solution.py:113
  54.8 20.6 %all-to-all-start.2 = ((f32[16,40,128]{2,1,0:T(8,128)}), f32[16,40,128]{2,1,0:T(8,128)S(1)}, u32[]{:S(2)}, u32[]{:S(2)}) async-start(f32[16,40,128]{2,1,0:T(8,128)} %get-tuple-element.31), calls=%async_computation.2 | async-start | bytes 655360 | tf_op jit(solution)/shard_map/all_to_all | solution.py:120
  58.3 1.3 collective-permute-start.1
  59.6 5.0 %collective-permute-start.4 = (f32[32,256]{1,0:T(8,128)S(1)}, f32[32,256]{1,0:T(8,128)S(1)}, u32[]{:S(2)}, u32[]{:S(2)}) collective-permute-start(f32[32,256]{1,0:T(8,128)S(1)} %add.3.refs_0_), channel_id=1, source_target_pairs={{0,6},{2,4},{4,2},{6,0},{8,14},{10,12},{12,10},{14,8},{16,22},{18,... | collective-permute-start | bytes 98312 | tf_op jit(solution)/shard_map/ppermute | solution.py:113
  62.3 4.1 %collective-permute-start.3 = (f32[32,256]{1,0:T(8,128)S(1)}, f32[32,256]{1,0:T(8,128)S(1)}, u32[]{:S(2)}, u32[]{:S(2)}) collective-permute-start(f32[32,256]{1,0:T(8,128)S(1)} %add.3.refs_0_), channel_id=1, source_target_pairs={{0,4},{2,6},{4,0},{6,2},{8,12},{10,14},{12,8},{14,10},{16,20},{18,... | collective-permute-start | bytes 98312 | tf_op jit(solution)/shard_map/ppermute | solution.py:113
  62.9 3.9 %collective-permute-start.2 = (f32[32,256]{1,0:T(8,128)S(1)}, f32[32,256]{1,0:T(8,128)S(1)}, u32[]{:S(2)}, u32[]{:S(2)}) collective-permute-start(f32[32,256]{1,0:T(8,128)S(1)} %add.3.refs_0_), channel_id=1, source_target_pairs={{0,2},{2,0},{4,6},{6,4},{8,10},{10,8},{12,14},{14,12},{16,18},{18,... | collective-permute-start | bytes 98312 | tf_op jit(solution)/shard_map/ppermute | solution.py:113
  66.8 6.4 %collective-permute-start.7 = (f32[32,256]{1,0:T(8,128)S(1)}, f32[32,256]{1,0:T(8,128)S(1)}, u32[]{:S(2)}, u32[]{:S(2)}) collective-permute-start(f32[32,256]{1,0:T(8,128)S(1)} %add.4.refs_0_), channel_id=1, source_target_pairs={{0,24},{2,26},{4,28},{6,30},{8,16},{10,18},{12,20},{14,22},{16,8},... | collective-permute-start | bytes 98312 | tf_op jit(solution)/shard_map/ppermute | solution.py:113
  70.6 4.8 %collective-permute-start.6 = (f32[32,256]{1,0:T(8,128)S(1)}, f32[32,256]{1,0:T(8,128)S(1)}, u32[]{:S(2)}, u32[]{:S(2)}) collective-permute-start(f32[32,256]{1,0:T(8,128)S(1)} %add.4.refs_0_), channel_id=1, source_target_pairs={{0,16},{2,18},{4,20},{6,22},{8,24},{10,26},{12,28},{14,30},{16,0},... | collective-permute-start | bytes 98312 | tf_op jit(solution)/shard_map/ppermute | solution.py:113
  70.6 4.8 %collective-permute-start.5 = (f32[32,256]{1,0:T(8,128)S(1)}, f32[32,256]{1,0:T(8,128)S(1)}, u32[]{:S(2)}, u32[]{:S(2)}) collective-permute-start(f32[32,256]{1,0:T(8,128)S(1)} %add.4.refs_0_), channel_id=1, source_target_pairs={{0,8},{2,10},{4,12},{6,14},{8,0},{10,2},{12,4},{14,6},{16,24},{18,... | collective-permute-start | bytes 98312 | tf_op jit(solution)/shard_map/ppermute | solution.py:113
  81.8 2.8 %collective-permute-start.8 = (f32[128,2176]{1,0:T(8,128)S(1)}, f32[128,2176]{1,0:T(8,128)S(1)}, u32[]{:S(2)}, u32[]{:S(2)}) collective-permute-start(f32[128,2176]{1,0:T(8,128)S(1)} %get-tuple-element.37.refs_0_), channel_id=1, source_target_pairs={{0,1},{1,0},{2,3},{3,2},{4,5},{5,4},{6,7},{7,6},{8,9},{9,8},{10,11... | collective-permute-start | bytes 3342344 | tf_op jit(solution)/shard_map/ppermute | solution.py:113
  84.7 1.0 copy-start.5
  90.8 25.2 %all-to-all-start.3 = ((f32[16,32,128]{2,1,0:T(8,128)}), f32[16,32,128]{2,1,0:T(8,128)S(1)}, u32[]{:S(2)}, u32[]{:S(2)}) async-start(f32[16,32,128]{2,1,0:T(8,128)} %get-tuple-element.38), calls=%async_computation.3 | async-start | bytes 524288 | tf_op jit(solution)/shard_map/all_to_all | solution.py:120
  95.1 5.6 %collective-permute-start.11 = (f32[32,256]{1,0:T(8,128)S(1)}, f32[32,256]{1,0:T(8,128)S(1)}, u32[]{:S(2)}, u32[]{:S(2)}) collective-permute-start(f32[32,256]{1,0:T(8,128)S(1)} %get-tuple-element.40.refs_0_), channel_id=1, source_target_pairs={{0,6},{2,4},{4,2},{6,0},{8,14},{10,12},{12,10},{14,8},{16,22},{18,... | collective-permute-start | bytes 98312 | tf_op jit(solution)/shard_map/ppermute | solution.py:113
  98.0 4.1 %collective-permute-start.10 = (f32[32,256]{1,0:T(8,128)S(1)}, f32[32,256]{1,0:T(8,128)S(1)}, u32[]{:S(2)}, u32[]{:S(2)}) collective-permute-start(f32[32,256]{1,0:T(8,128)S(1)} %get-tuple-element.40.refs_0_), channel_id=1, source_target_pairs={{0,4},{2,6},{4,0},{6,2},{8,12},{10,14},{12,8},{14,10},{16,20},{18,... | collective-permute-start | bytes 98312 | tf_op jit(solution)/shard_map/ppermute | solution.py:113
  98.5 3.9 %collective-permute-start.9 = (f32[32,256]{1,0:T(8,128)S(1)}, f32[32,256]{1,0:T(8,128)S(1)}, u32[]{:S(2)}, u32[]{:S(2)}) collective-permute-start(f32[32,256]{1,0:T(8,128)S(1)} %get-tuple-element.40.refs_0_), channel_id=1, source_target_pairs={{0,2},{2,0},{4,6},{6,4},{8,10},{10,8},{12,14},{14,12},{16,18},{18,... | collective-permute-start | bytes 98312 | tf_op jit(solution)/shard_map/ppermute | solution.py:113
  102.5 5.8 %collective-permute-start.14 = (f32[32,256]{1,0:T(8,128)S(1)}, f32[32,256]{1,0:T(8,128)S(1)}, u32[]{:S(2)}, u32[]{:S(2)}) collective-permute-start(f32[32,256]{1,0:T(8,128)S(1)} %add.5.refs_0_), channel_id=1, source_target_pairs={{0,24},{2,26},{4,28},{6,30},{8,16},{10,18},{12,20},{14,22},{16,8},... | collective-permute-start | bytes 98312 | tf_op jit(solution)/shard_map/ppermute | solution.py:113
  106.1 4.8 %collective-permute-start.13 = (f32[32,256]{1,0:T(8,128)S(1)}, f32[32,256]{1,0:T(8,128)S(1)}, u32[]{:S(2)}, u32[]{:S(2)}) collective-permute-start(f32[32,256]{1,0:T(8,128)S(1)} %add.5.refs_0_), channel_id=1, source_target_pairs={{0,16},{2,18},{4,20},{6,22},{8,24},{10,26},{12,28},{14,30},{16,0},... | collective-permute-start | bytes 98312 | tf_op jit(solution)/shard_map/ppermute | solution.py:113
  106.1 4.8 %collective-permute-start.12 = (f32[32,256]{1,0:T(8,128)S(1)}, f32[32,256]{1,0:T(8,128)S(1)}, u32[]{:S(2)}, u32[]{:S(2)}) collective-permute-start(f32[32,256]{1,0:T(8,128)S(1)} %add.5.refs_0_), channel_id=1, source_target_pairs={{0,8},{2,10},{4,12},{6,14},{8,0},{10,2},{12,4},{14,6},{16,24},{18,... | collective-permute-start | bytes 98312 | tf_op jit(solution)/shard_map/ppermute | solution.py:113
